TPU v7x, 32 devices: a whole 2x2x4 slice. The times are simulated.
32 devices in a mesh: ctx: 8 (over z, x), exp: 4 (over y, core).
Axes of the slice: x: 2, y: 2, z: 4, core: 2. Of those that a mesh axis runs over, the one named last changes fastest.
Arguments:
- q_spikes: bfloat16 [4096, 4096], P('ctx', 'exp'), may hold values from -1 to 1, as said below
- k_spikes: bfloat16 [4096, 4096], P('ctx', 'exp'), may hold values from -1 to 1, as said below
- v_spikes: bfloat16 [4096, 4096], P('ctx', 'exp'), may hold values from -1 to 1, as said below
- log_decay: float32 [4096, 32], P('ctx', 'exp'), may hold values from -1 to 0, as said below
- norm_gain: float32 [4096], P('exp'), may hold values from 0.1 to 1.9
- out_weight: bfloat16 [4096, 4096], P('exp'), may hold values from -0.09375 to 0.09375
- residual: bfloat16 [4096, 4096], P(('ctx', 'exp')), may hold values from -6 to 6
Outputs:
- mixed: bfloat16 [4096, 4096], P(('ctx', 'exp'))
Inputs may be any that keep to these rules, and one draw needn't show every extreme that they name: `q_spikes`: every entry is -1, 0 or 1. `k_spikes`: every entry is -1, 0 or 1. `v_spikes`: every entry is -1, 0 or 1. `log_decay`: every entry is negative.
All inputs are finite; a program needn't handle non-finite values.
Results may differ from a plain program's by a relative error of at most 0.015.
Values may be sent and summed in bfloat16 or wider, within the bound.
No kernel may reach another device: no remote copies, remote signals or barrier semaphores. Data moves between devices by JAX's collectives and lax.ppermute only.
A program may use at most 64 MiB of HBM per device.

v0:
```python
import jax
import jax.numpy as jnp
from jax import lax
from jax.sharding import PartitionSpec as P

HIGH = lax.Precision.HIGHEST


def entering(shard, axis, join, neutral):
    place = lax.axis_index(axis)
    gathered = jax.tree.map(
        lambda a, kind: lax.all_gather(a.astype(kind), axis), shard, (jnp.bfloat16, jnp.bfloat16)
    )
    state = jax.tree.map(lambda a, e: jnp.zeros_like(a) + jnp.asarray(e, a.dtype), shard, neutral)

    def one(lap, state):
        return join(
            state,
            jax.tree.map(
                lambda a, own: lax.dynamic_index_in_dim(a, lap, 0, False).astype(own.dtype),
                gathered,
                shard,
            ),
        )

    return lax.fori_loop(0, place, one, state)


def shards(q_spikes, k_spikes, v_spikes, log_decay, norm_gain, out_weight, residual):
    rows = q_spikes.shape[0]
    heads = log_decay.shape[1]
    width = q_spikes.shape[1] // heads
    query = q_spikes.astype(jnp.float32).reshape(rows, heads, width)
    key = k_spikes.astype(jnp.float32).reshape(rows, heads, width)
    value = v_spikes.astype(jnp.float32).reshape(rows, heads, width)
    cum = jnp.cumsum(log_decay, axis=0)
    place = jnp.arange(rows)
    causal = place[:, None] >= place[None, :]
    spread = cum[:, None, :] - cum[None, :, :]
    weight = jnp.exp(jnp.where(causal[:, :, None], spread, -jnp.inf))
    scores = jnp.einsum("thd,shd->tsh", query, key, precision=HIGH) * weight
    local = jnp.einsum("tsh,she->the", scores, value, precision=HIGH)
    total = cum[-1]
    keyed = key * jnp.exp(total[None, :] - cum)[:, :, None]
    own_state = jnp.einsum("shd,she->hde", keyed, value, precision=HIGH)
    empty = jnp.zeros((heads, width, width), jnp.float32)

    def combine(earlier, later):
        return (earlier[0] + later[0], earlier[1] * jnp.exp(later[0])[:, None, None] + later[1])

    decay_in, state_in = entering(
        (total, own_state), "ctx", combine, (jnp.zeros((heads,), jnp.float32), empty)
    )
    carried = jnp.einsum("thd,hde->the", query, state_in, precision=HIGH) * jnp.exp(cum)[:, :, None]
    attended = local + carried
    scale = jnp.sqrt(jnp.mean(attended * attended, axis=-1, keepdims=True) + 1e-06)
    normed = (
        (attended / scale * norm_gain.reshape(heads, width))
        .astype(jnp.bfloat16)
        .reshape(rows, heads * width)
    )
    summed = lax.psum_scatter(
        jnp.dot(normed, out_weight, preferred_element_type=jnp.float32).astype(jnp.bfloat16),
        "exp",
        scatter_dimension=0,
        tiled=True,
    ).astype(jnp.float32)
    return (summed + residual.astype(jnp.float32)).astype(jnp.bfloat16)


def solution(mesh):
    in_specs = (
        P("ctx", "exp"),
        P("ctx", "exp"),
        P("ctx", "exp"),
        P("ctx", "exp"),
        P("exp"),
        P("exp", None),
        P(("ctx", "exp"), None),
    )
    out_specs = P(("ctx", "exp"), None)
    return jax.shard_map(shards, mesh=mesh, in_specs=in_specs, out_specs=out_specs, check_vma=False)
```

profile of v0, /device:TPU:24, one launch (start us, length us, event | category | flops | bytes accessed | tf_op | source)
XLA Modules:
  0.0 137.9 jit_solution(7855345486980600610)
XLA Ops:
  6.5 0.0 copy-start
  6.5 0.0 all-gather.4.cloned.1.call-start
  6.5 2.3 %reduce-window.6 = f32[8,4,128]{2,0,1:T(8,128)S(1)} reduce-window(f32[8,4,128]{2,0,1:T(8,128)} %bitcast.68, f32[]{:T(128)} %constant.30.clone.1), window={size=1x1x128 pad=0_0x0_0x127_0}, to_apply=%region_0.0 | reduce-window | flops 520192 | bytes 32772 | tf_op jit(solution)/shard_map/reduce-window
  8.8 0.2 slice_reduce_fusion
  9.0 0.1 fusion.27
  9.1 0.2 slice_reduce_fusion.1
  9.3 0.1 subtract_exponential_fusion
  9.4 1.5 %copy.41 = bf16[512,1024]{0,1:T(8,128)(2,1)S(1)} copy(bf16[512,1024]{1,0:T(8,128)(2,1)} %param.10) | data formatting | bytes 2097152 | tf_op jit(solution)/shard_map/reshape | solution.py:34
  10.9 3.2 %fusion.12 = bf16[8,128,128]{2,1,0:T(8,128)(2,1)} fusion(bf16[512,8,128]{0,2,1:T(8,128)(2,1)S(1)} %bitcast.64, f32[512,8]{0,1:T(8,128)S(1)} %subtract_exponential_fusion, bf16[512,1024]{1,0:T(8,128)(2,1)} %param.11), kind=kOutput, calls=%fused_computation.20 | convolution fusion | flops 806486016 | bytes 2375680 | tf_op jit(solution)/shard_map/shd,she->hde/dot_general | solution.py:45
  14.1 0.0 all-gather.4.cloned.1.call-update
  14.1 0.0 reduce-scatter.2.cloned.1.call-start
  14.2 0.2 fusion.25
  14.4 15.9 %all-gather.1 = bf16[8,1,8]{2,1,0:T(2,128)(2,1)S(1)} all-gather(bf16[1,1,8]{2,1,0:T(2,128)(2,1)S(1)} %bitcast.71), channel_id=1, replica_groups=mesh['ctx'=8,'exp'=4] {'ctx'}, dimensions={0}, use_global_device_ids=true | all-gather | bytes 144 | tf_op jit(solution)/shard_map/all_gather | solution.py:12
  30.3 0.1 iota_compare_fusion
  30.4 0.0 copy-done
  30.4 0.0 copy-start.3
  30.4 1.3 fusion.18
  31.7 0.0 copy-done.3
  31.7 6.5 %fusion = f32[8,512,128]{1,2,0:T(8,128)} fusion(f32[8,512,512]{2,1,0:T(8,128)S(1)} %fusion.18, f32[512,8]{0,1:T(8,128)S(1)} %get-tuple-element.61, pred[512,512]{0,1:T(8,128)(4,1)S(1)} %iota_compare_fusion, bf16[512,1024]{1,0:T(8,128)(2,1)S(1)} %copy-done.3), kind=kOutput, calls=%fused_computation.3 | convolution fusion | flops 3227516928 | bytes 11812864 | tf_op jit(solution)/shard_map/tsh,she->the/dot_general | solution.py:42
  38.2 24.8 %all-gather.4.cloned.1.call-done = bf16[64,128,128]{2,1,0:T(8,128)(2,1)} async-done(((bf16[8,128,128]{2,1,0:T(8,128)(2,1)}), bf16[64,128,128]{2,1,0:T(8,128)(2,1)}) %all-gather.4.cloned.1.call-update) | async-done | bytes 2097168 | tf_op jit(solution)/shard_map/all_gather | solution.py:12
  63.1 6.9 %while.12 = (s32[]{:T(128)}, f32[8,128,128]{2,1,0:T(8,128)S(1)}, s32[]{:T(128)}, bf16[8,8]{1,0:T(8,128)(2,1)S(1)}, bf16[8,8,128,128]{3,2,1,0:T(8,128)(2,1)}, /*index=5*/s32[]{:T(128)}, s32[]{:T(128)}, s32[]{:T(128)}) while((s32[]{:T(128)}, f32[8,128,128]{2,1,0:T(8,128)S(1)}, s32[]{:T(128)}, bf16[8,8]{1,0:T(8,128)(2,1)S(1)}, ...), condition=%wide.region_3.4_spmd, body=%wide.region_2.3_spmd.sunk | while | flops 393229 | bytes 1310935 | solution.py:26
  63.1 1.1 convert_add_fusion.2
  64.3 1.1 convert_add_fusion.2
  65.4 1.1 convert_add_fusion.2
  66.6 1.1 convert_add_fusion.2
  67.7 1.1 convert_add_fusion.2
  68.9 1.1 convert_add_fusion.2
  70.0 0.0 copy-start.2
  70.0 2.9 %multiply_reduce_fusion = (f32[512,8]{0,1:T(8,128)S(1)}, f32[512,8,128]{0,2,1:T(8,128)S(1)}) fusion(f32[512,8]{0,1:T(8,128)S(1)} %get-tuple-element.60, f32[8,128,128]{2,1,0:T(8,128)S(1)} %get-tuple-element.49, f32[8,512,128]{1,2,0:T(8,128)} %fusion, bf16[512,1024]{1,0:T(8,128)(2,1)S(1)} %copy-done), kind=kOutput, calls=%fused_computation.16 | convolution fusion | flops 807399424 | bytes 5799936 | tf_op jit(solution)/shard_map/thd,hde->the/dot_general | solution.py:54
  72.9 0.0 copy-done.2
  72.9 0.3 multiply_convert_fusion
  73.2 9.5 %convolution_convert_fusion = bf16[512,4096]{1,0:T(8,128)(2,1)} fusion(bf16[512,1024]{0,1:T(8,128)(2,1)S(1)} %bitcast.66, bf16[1024,4096]{1,0:T(8,128)(2,1)} %param.14), kind=kOutput, calls=%fused_computation.7 | convolution fusion | flops 4297064448 | bytes 13631488 | tf_op jit(solution)/shard_map/dot_general | solution.py:63
  82.7 0.0 copy-start.1
  82.7 0.0 reduce-scatter.2.cloned.1.call-update
  82.7 45.9 %reduce-scatter.2.cloned.1.call-done = bf16[128,4096]{1,0:T(8,128)(2,1)} async-done(((bf16[512,4096]{1,0:T(8,128)(2,1)}), bf16[128,4096]{1,0:T(8,128)(2,1)}) %reduce-scatter.2.cloned.1.call-update) | async-done | bytes 1048592 | tf_op jit(solution)/shard_map/reduce_scatter | solution.py:62
  128.6 0.0 copy-done.1
  128.6 2.4 %add_convert_fusion = bf16[128,4096]{1,0:T(8,128)(2,1)} fusion(bf16[128,4096]{1,0:T(8,128)(2,1)S(1)} %copy-done.1, bf16[128,4096]{1,0:T(8,128)(2,1)} %reduce-scatter.2.cloned.1.call-done), kind=kLoop, calls=%fused_computation.14 | loop fusion | flops 2097152 | bytes 3145728 | tf_op jit(solution)/shard_map/convert_element_type | solution.py:68
  (11 shorter events, 0.2 us)
Async XLA Ops:
  6.5 23.9 %copy-start = (bf16[512,1024]{1,0:T(8,128)(2,1)S(1)}, bf16[512,1024]{1,0:T(8,128)(2,1)}, u32[]{:S(2)}) copy-start(bf16[512,1024]{1,0:T(8,128)(2,1)} %param.9) | copy-start | bytes 3145732
  6.5 56.5 %all-gather.4.cloned.1.call-start = ((), (), s32[]{:S(2)}) async-start(), calls=%async_computation.2 | async-start | bytes 2359296 | tf_op jit(solution)/shard_map/all_gather | solution.py:12
  14.1 114.5 %reduce-scatter.2.cloned.1.call-start = ((), (), s32[]{:S(2)}) async-start(), calls=%async_computation.1 | async-start | bytes 5242880 | tf_op jit(solution)/shard_map/reduce_scatter | solution.py:62
  30.4 1.3 copy-start.3
  70.0 2.9 %copy-start.2 = (f32[1024]{0:T(1024)S(1)}, f32[1024]{0:T(1024)}, u32[]{:S(2)}) copy-start(f32[1024]{0:T(1024)} %param.13) | copy-start | bytes 12292
  82.7 45.9 %copy-start.1 = (bf16[128,4096]{1,0:T(8,128)(2,1)S(1)}, bf16[128,4096]{1,0:T(8,128)(2,1)}, u32[]{:S(2)}) copy-start(bf16[128,4096]{1,0:T(8,128)(2,1)} %param.15) | copy-start | bytes 3145732
Sparse Core Ops, SparseCore 0:
  14.2 48.7 all-gather.3
  82.9 45.7 reduce-scatter.1
where the time goes:
time: 140 us; the launch traced here: 138 us
  waiting for transfers between devices  70.7 us (50%)
  matrix products  23.3 us (17%)
  blocking collectives  15.9 us (11%)
  between operations  13.5 us (10%)
  other arithmetic  12.1 us (9%)
  local copies, waits for them, and re-layouts  2.09 us (1%)
    reduce_scatter x1, waiting for transfers between devices, shards(): lax.psum_scatter(jnp.dot(normed, out_weight, preferred_element_type=jnp.f...  45.9 us
    all_gather x1, waiting for transfers between devices, entering(): lax.all_gather(a.astype(kind), axis)  24.8 us
    all_gather x1, blocking collectives, entering(): lax.all_gather(a.astype(kind), axis)  15.9 us
    dot_general x1, matrix products, shards(): jnp.dot(normed, out_weight, preferred_element_type=jnp.float32)  9.48 us
    add x6, other arithmetic, combine(): earlier[1] * jnp.exp(later[0])[:, None, None] + later[1]  6.66 us
    dot_general x1, matrix products, shards(): local = jnp.einsum('tsh,she->the', scores, value, precision=HIGH)  6.47 us
    dot_general x1, matrix products, shards(): own_state = jnp.einsum('shd,she->hde', keyed, value, precision=HIGH)  3.2 us
    dot_general x1, matrix products, shards(): jnp.einsum('thd,hde->the', query, state_in, precision=HIGH)  2.88 us
  transfers between devices with their start and end apart: 2, of which 2 were waited for; matrix products, arithmetic and copies ran while one was open for 6% of the time, Pallas kernels for 0%

commit v1 on v0

v1 whole, which is shorter than its diff:
```python
import functools

import jax
import jax.numpy as jnp
from jax import lax
from jax.experimental import pallas as pl
from jax.experimental.pallas import tpu as pltpu
from jax.sharding import PartitionSpec as P

HIGH = lax.Precision.HIGHEST
F32 = jnp.float32
BF16 = jnp.bfloat16


def tile_of(size, want):
    while size % want:
        want //= 2
    return want


def pad_rows(half):
    return -(-half // 8) * 8


def running_sum(logd):
    rows = logd.shape[0]
    tile = tile_of(rows, 128)
    lower = (
        lax.broadcasted_iota(jnp.int32, (tile, tile), 0)
        >= lax.broadcasted_iota(jnp.int32, (tile, tile), 1)
    ).astype(F32)
    done, carry = [], None
    for i in range(rows // tile):
        part = jnp.dot(
            lower, logd[i * tile : (i + 1) * tile], precision=HIGH, preferred_element_type=F32
        )
        if carry is not None:
            part = part + carry
        carry = part[tile - 1 : tile]
        done.append(part)
    return jnp.concatenate(done, axis=0)


def state_kernel(half, width, which_ref, logd_ref, key_ref, value_ref, pay_ref, cum_ref):
    second = which_ref[0] == 1
    cum = running_sum(logd_ref[...])
    cum_ref[...] = cum
    rows = cum.shape[0]
    narrow = pay_ref.dtype == BF16
    pad = pad_rows(half)
    base = half * width
    pay_ref[base:, :] = jnp.zeros((2 * pad, width), pay_ref.dtype)
    highs, lows = [], []
    for j in range(half):
        mine = jnp.where(second, cum[:, half + j : half + j + 1], cum[:, j : j + 1])
        total = mine[rows - 1 : rows]
        weight = jnp.exp(total - mine)
        cols = slice(j * width, (j + 1) * width)
        keyed = (key_ref[:, cols].astype(F32) * weight).astype(BF16)
        state = lax.dot_general(
            keyed, value_ref[:, cols], (((0,), (0,)), ((), ())), preferred_element_type=F32
        )
        pay_ref[j * width : (j + 1) * width, :] = state.astype(pay_ref.dtype)
        decay = jnp.broadcast_to(jnp.exp(total), (1, width))
        if narrow:
            high = decay.astype(BF16).astype(F32)
            highs.append(high)
            lows.append(decay - high)
        else:
            highs.append(decay)
            lows.append(jnp.zeros_like(decay))
    blank = [jnp.zeros((1, width), F32)] * (pad - half)
    tail = jnp.concatenate(highs + blank + lows + blank, axis=0)
    pay_ref[base:, :] = tail.astype(pay_ref.dtype)


def states(which, logd, key, value, half, width, kind):
    rows, heads = logd.shape
    cols = half * width
    tall = cols + 2 * pad_rows(half)
    return pl.pallas_call(
        functools.partial(state_kernel, half, width),
        grid_spec=pltpu.PrefetchScalarGridSpec(
            num_scalar_prefetch=1,
            grid=(1,),
            in_specs=[
                pl.BlockSpec((rows, heads), lambda i, w: (0, 0)),
                pl.BlockSpec((rows, cols), lambda i, w: (0, w[0])),
                pl.BlockSpec((rows, cols), lambda i, w: (0, w[0])),
            ],
            out_specs=[
                pl.BlockSpec((tall, width), lambda i, w: (0, 0)),
                pl.BlockSpec((rows, heads), lambda i, w: (0, 0)),
            ],
        ),
        out_shape=[
            jax.ShapeDtypeStruct((tall, width), kind),
            jax.ShapeDtypeStruct((rows, heads), F32),
        ],
        name="states",
    )(which, logd, key, value)


def local_kernel(half, width, part, cum_ref, across_ref, q_ref, k_ref, v_ref, out_ref):
    rows = cum_ref.shape[0]
    tile = tile_of(rows, 256)
    for j in range(half):
        head = part * half + j
        cols = slice(j * width, (j + 1) * width)
        for i in range(rows // tile):
            here = slice(i * tile, (i + 1) * tile)
            upto = slice(0, (i + 1) * tile)
            scores = lax.dot_general(
                q_ref[here, cols],
                k_ref[upto, cols],
                (((1,), (1,)), ((), ())),
                preferred_element_type=F32,
            )
            shape = scores.shape
            spread = cum_ref[here, head : head + 1] - across_ref[head : head + 1, upto]
            causal = (
                lax.broadcasted_iota(jnp.int32, shape, 0) + i * tile
                >= lax.broadcasted_iota(jnp.int32, shape, 1)
            )
            weight = jnp.exp(jnp.where(causal, spread, -jnp.inf))
            out_ref[here, cols] = jnp.dot(
                (scores * weight).astype(BF16), v_ref[upto, cols], preferred_element_type=F32
            )


def local(cum, across, query, key, value, half, width, part):
    rows, heads = cum.shape
    cols = half * width
    block = pl.BlockSpec((rows, cols), lambda i: (0, part))
    return pl.pallas_call(
        functools.partial(local_kernel, half, width, part),
        grid=(1,),
        in_specs=[
            pl.BlockSpec((rows, heads), lambda i: (0, 0)),
            pl.BlockSpec((heads, rows), lambda i: (0, 0)),
            block,
            block,
            block,
        ],
        out_specs=pl.BlockSpec((rows, cols), lambda i: (0, 0)),
        out_shape=jax.ShapeDtypeStruct((rows, cols), F32),
        name="local",
    )(cum, across, query, key, value)


def norm_kernel(half, width, spot_ref, cum_ref, q_ref, one_ref, two_ref, low_ref, high_ref, gain_ref, out_ref):
    for head in range(2 * half):
        cols = slice(head * width, (head + 1) * width)
        j = head % half
        near = slice(j * width, (j + 1) * width)
        inside, state = (one_ref, low_ref) if head < half else (two_ref, high_ref)
        carried = jnp.dot(q_ref[:, cols], state[near, :], preferred_element_type=F32)
        attended = inside[:, near] + carried * jnp.exp(cum_ref[:, head : head + 1])
        square = jnp.mean(attended * attended, axis=-1, keepdims=True)
        out_ref[:, cols] = (
            attended * lax.rsqrt(square + 1e-06) * gain_ref[:, cols]
        ).astype(out_ref.dtype)


def norm(spot, cum, query, one, two, low, high, gain, half, width, chips, away):
    rows, heads = cum.shape
    block = rows // (2 * chips)
    cols = heads * width

    def at(i, s):
        return 2 * lax.rem(s[0] + i, chips) + (1 - s[1] if away else s[1])

    whole = pl.BlockSpec((half * width, width), lambda i, s: (0, 0))
    return pl.pallas_call(
        functools.partial(norm_kernel, half, width),
        grid_spec=pltpu.PrefetchScalarGridSpec(
            num_scalar_prefetch=1,
            grid=(chips,),
            in_specs=[
                pl.BlockSpec((block, heads), lambda i, s: (at(i, s), 0)),
                pl.BlockSpec((block, cols), lambda i, s: (at(i, s), 0)),
                pl.BlockSpec((block, half * width), lambda i, s: (at(i, s), 0)),
                pl.BlockSpec((block, half * width), lambda i, s: (at(i, s), 0)),
                whole,
                whole,
                pl.BlockSpec((1, cols), lambda i, s: (0, 0)),
            ],
            out_specs=pl.BlockSpec((block, cols), lambda i, s: (i, 0)),
        ),
        out_shape=jax.ShapeDtypeStruct((chips * block, cols), BF16),
        name="norm_away" if away else "norm_home",
    )(spot, cum, query, one, two, low, high, gain)


def project_kernel(block, mine_ref, other_ref, near_ref, far_ref, own_ref, away_ref):
    total = jnp.dot(mine_ref[...], near_ref[...], preferred_element_type=F32) + jnp.dot(
        other_ref[...], far_ref[...], preferred_element_type=F32
    )
    own_ref[...] = total[:block]
    away_ref[...] = total[block:].astype(away_ref.dtype)


def project(mine, other, near, far, block, first, count, tile):
    rows, depth = mine.shape
    start = first // tile
    return pl.pallas_call(
        functools.partial(project_kernel, block),
        grid=(count // tile,),
        in_specs=[
            pl.BlockSpec((rows, depth), lambda i: (0, 0)),
            pl.BlockSpec((rows, depth), lambda i: (0, 0)),
            pl.BlockSpec((depth, tile), lambda i: (0, start + i)),
            pl.BlockSpec((depth, tile), lambda i: (0, start + i)),
        ],
        out_specs=[
            pl.BlockSpec((block, tile), lambda i: (0, i)),
            pl.BlockSpec((rows - block, tile), lambda i: (0, i)),
        ],
        out_shape=[
            jax.ShapeDtypeStruct((block, count), F32),
            jax.ShapeDtypeStruct((rows - block, count), BF16),
        ],
        name="project",
    )(mine, other, near, far)


def unpack(pay, half, width):
    pay = pay.astype(F32)
    base, pad = half * width, pad_rows(half)
    state = pay[:base].reshape(half, width, width)
    decay = pay[base : base + half, :1] + pay[base + pad : base + pad + half, :1]
    return state, decay.reshape(half, 1, 1)


def pack(state, decay):
    half, width, _ = state.shape
    pad = pad_rows(half)
    decay = decay.reshape(half, 1)
    high = lax.reduce_precision(decay, 8, 7)
    low = decay - high

    def spread(a):
        return jnp.pad(jnp.broadcast_to(a.astype(BF16), (half, width)), ((0, pad - half), (0, 0)))

    return jnp.concatenate(
        [state.astype(BF16).reshape(half * width, width), spread(high), spread(low)], axis=0
    )


def shards(blocks, group, q_spikes, k_spikes, v_spikes, log_decay, norm_gain, out_weight, residual):
    rows, heads = log_decay.shape
    width = q_spikes.shape[1] // heads
    half = heads // 2
    chips = group // 2
    block = rows // group
    place = lax.axis_index("ctx")
    member = lax.axis_index("exp")
    side = place % 2
    is_first = side == 0
    swap = [(i, i ^ 1) for i in range(blocks)]
    cores = [(i, i ^ 1) for i in range(group)]

    def which(a):
        return a.astype(jnp.int32).reshape(1)

    sent, cum = states(which(1 - side), log_decay, k_spikes, v_spikes, half, width, BF16)
    met = lax.ppermute(sent, "ctx", swap)
    far_weight = lax.ppermute(out_weight, "exp", cores)
    kept, _ = states(which(side), log_decay, k_spikes, v_spikes, half, width, F32)
    across = cum.T
    one = local(cum, across, q_spikes, k_spikes, v_spikes, half, width, 0)
    two = local(cum, across, q_spikes, k_spikes, v_spikes, half, width, 1)

    own_state, own_decay = unpack(kept, half, width)
    met_state, met_decay = unpack(met, half, width)
    first = jnp.where(is_first, own_state, met_state)
    second = jnp.where(is_first, met_state, own_state)
    first_decay = jnp.where(is_first, own_decay, met_decay)
    second_decay = jnp.where(is_first, met_decay, own_decay)
    window, window_decay = first * second_decay + second, first_decay * second_decay
    before, before_decay = jnp.zeros_like(window), jnp.ones_like(window_decay)
    step = 1
    while 2 * step < blocks:
        got = lax.ppermute(
            pack(window, window_decay), "ctx", [(i, i + 2 * step) for i in range(blocks - 2 * step)]
        )
        got, got_decay = unpack(got, half, width)
        before, before_decay = got * before_decay + before, got_decay * before_decay
        window, window_decay = got * window_decay + window, got_decay * window_decay
        step *= 2
    after = before * first_decay + first
    mine = jnp.where(is_first, before, after).astype(BF16).reshape(half * width, width)
    theirs = jnp.where(is_first, after, before).astype(BF16).reshape(half * width, width)
    got = lax.ppermute(theirs, "ctx", swap)
    low = jnp.where(is_first, mine, got)
    high = jnp.where(is_first, got, mine)

    spot = jnp.stack([member // 2, member % 2]).astype(jnp.int32)
    gain = norm_gain.reshape(1, heads * width)
    args = (spot, cum, q_spikes, one, two, low, high, gain, half, width, chips)
    away = norm(*args, True)
    other = lax.ppermute(away, "exp", cores)
    home = norm(*args, False)

    total = out_weight.shape[1]
    tile = tile_of(total, 512)
    chunk = max(tile, total // 4)
    done = []
    for at in range(0, total, chunk):
        own, parts = project(home, other, out_weight, far_weight, block, at, chunk, tile)
        summed = own + residual[:, at : at + chunk].astype(F32)
        for d in range(1, chips):
            part = parts[(d - 1) * block : d * block]
            perm = [(i, 2 * ((i // 2 + d) % chips) + i % 2) for i in range(group)]
            summed = summed + lax.ppermute(part, "exp", perm).astype(F32)
        done.append(summed.astype(BF16))
    return jnp.concatenate(done, axis=1)


def solution(mesh):
    in_specs = (
        P("ctx", "exp"),
        P("ctx", "exp"),
        P("ctx", "exp"),
        P("ctx", "exp"),
        P("exp"),
        P("exp", None),
        P(("ctx", "exp"), None),
    )
    out_specs = P(("ctx", "exp"), None)
    return jax.shard_map(
        functools.partial(shards, mesh.shape["ctx"], mesh.shape["exp"]),
        mesh=mesh,
        in_specs=in_specs,
        out_specs=out_specs,
        check_vma=False,
    )
```

time: 140 us -> 87.6 us (0.63); the launches traced: 138 us -> 87 us
  waiting for transfers between devices: 70.7 us -> 24.9 us
  Pallas kernels: 0 us -> 38.7 us
  matrix products: 23.3 us -> 0 us
  blocking collectives: 15.9 us -> 0 us
  between operations: 13.5 us -> 0.14 us
  starting transfers between devices: 0.04 us -> 9.96 us
  other arithmetic: 12.1 us -> 9.88 us
    reduce_scatter x1 -> x0, waiting for transfers between devices: 45.9 us -> none  [shards(): lax.psum_scatter(jnp.dot(normed, out_weight, preferred_element_type=jnp.f...]
    pallas_call x0 -> x10, Pallas kernels: none -> 38.7 us  [the longest x4 16.2 us: project(): pl.pallas_call(functools.partial(project_kernel, block), grid=(count // t...]
    ppermute x0 -> x10, waiting for transfers between devices: none -> 24.9 us  [the longest x2 13.9 us: shards(): lax.ppermute(pack(window, window_decay), 'ctx', [(i, i + 2 * step) for i...]
    all_gather x1 -> x0, waiting for transfers between devices: 24.8 us -> none  [entering(): lax.all_gather(a.astype(kind), axis)]
    dot_general x5 -> x0, matrix products: 23.3 us -> none  [the longest x1 9.48 us: shards(): jnp.dot(normed, out_weight, preferred_element_type=jnp.float32)]
    all_gather x1 -> x0, blocking collectives: 15.9 us -> none  [entering(): lax.all_gather(a.astype(kind), axis)]
    ppermute x0 -> x10, starting transfers between devices: none -> 9.96 us  [the longest x4 4.31 us: shards(): summed = summed + lax.ppermute(part, 'exp', perm).astype(F32)]
    add x6 -> x1, other arithmetic: 6.66 us -> 0.12 us  [unpack(): decay = pay[base:base + half, :1] + pay[base + pad:base + pad + half, :1]]
  transfers between devices with their start and end apart: 2 -> 10, of which waited for: 2 -> 5; matrix products, arithmetic and copies ran while one was open for 6% -> 11% of each run, Pallas kernels for 0% -> 40%
where the time goes in v1:
time: 87.6 us; the launch traced here: 87 us
  Pallas kernels  38.7 us (44%)
  waiting for transfers between devices  24.9 us (28%)
  starting transfers between devices  9.96 us (11%)
  other arithmetic  9.88 us (11%)
  local copies, waits for them, and re-layouts  3.36 us (4%)
    pallas_call x4, Pallas kernels, project(): pl.pallas_call(functools.partial(project_kernel, block), grid=(count // t...  16.2 us
    ppermute x2, waiting for transfers between devices, shards(): lax.ppermute(pack(window, window_decay), 'ctx', [(i, i + 2 * step) for i...  13.9 us
    ppermute x4, waiting for transfers between devices, shards(): summed = summed + lax.ppermute(part, 'exp', perm).astype(F32)  9.35 us
    pallas_call x2, Pallas kernels, norm(): pl.pallas_call(functools.partial(norm_kernel, half, width), grid_spec=plt...  8.63 us
    pallas_call x2, Pallas kernels, local(): pl.pallas_call(functools.partial(local_kernel, half, width, part), grid=(...  7.81 us
    pallas_call x2, Pallas kernels, states(): pl.pallas_call(functools.partial(state_kernel, half, width), grid_spec=pl...  6.13 us
    ppermute x4, starting transfers between devices, shards(): summed = summed + lax.ppermute(part, 'exp', perm).astype(F32)  4.31 us
    ppermute x2, starting transfers between devices, shards(): lax.ppermute(pack(window, window_decay), 'ctx', [(i, i + 2 * step) for i...  2.58 us
  transfers between devices with their start and end apart: 10, of which 5 were waited for; matrix products, arithmetic and copies ran while one was open for 11% of the time, Pallas kernels for 40%

profile of v1, /device:TPU:24, one launch (start us, length us, event | category | flops | bytes accessed | tf_op | source)
XLA Modules:
  0.0 87.0 jit_solution(3747667332702638176)
XLA Ops:
  0.0 0.0 collective-permute-start.5
  0.0 1.6 %copy.11.logd_ref = f32[512,8]{1,0:T(8,128)} copy(f32[512,8]{0,1:T(8,128)} %param.10) | data formatting | bytes 32768 | tf_op args[3]
  1.6 3.0 %states.2 = (bf16[528,128]{1,0:T(8,128)(2,1)}, f32[512,8]{1,0:T(8,128)}) custom-call(s32[1]{0:T(128)} %bitcast.2.which_ref, f32[512,8]{1,0:T(8,128)} %copy.11.logd_ref, bf16[512,1024]{1,0:T(8,128)(2,1)} %key_ref.3, bf16[512,1024]{1,0:T(8,128)(2,1)} %value_ref.3), custom_call_target="tpu_custom_call" | custom-call | tf_op jit(solution)/shard_map/states/pallas_call | solution.py:81
  4.6 1.5 %collective-permute-start = (bf16[528,128]{1,0:T(8,128)(2,1)}, bf16[528,128]{1,0:T(8,128)(2,1)S(1)}, u32[]{:S(2)}, u32[]{:S(2)}) collective-permute-start(bf16[528,128]{1,0:T(8,128)(2,1)} %get-tuple-element.18), channel_id=1, source_target_pairs={{0,4},{4,0},{8,12},{12,8},{16,20},{20,16},{24,28},{28,24},{1,5},{5... | collective-permute-start | bytes 405512 | tf_op jit(solution)/shard_map/ppermute | solution.py:267
  6.1 3.1 %states.3 = (f32[528,128]{1,0:T(8,128)}, f32[512,8]{1,0:T(8,128)}) custom-call(s32[1]{0:T(128)} %bitcast.4.which_ref, f32[512,8]{1,0:T(8,128)} %copy.11.logd_ref, bf16[512,1024]{1,0:T(8,128)(2,1)} %key_ref.3, bf16[512,1024]{1,0:T(8,128)(2,1)} %value_ref.3), custom_call_target="tpu_custom_call" | custom-call | tf_op jit(solution)/shard_map/states/pallas_call | solution.py:81
  9.2 1.6 %collective-permute-done = bf16[528,128]{1,0:T(8,128)(2,1)S(1)} collective-permute-done((bf16[528,128]{1,0:T(8,128)(2,1)}, bf16[528,128]{1,0:T(8,128)(2,1)S(1)}, u32[]{:S(2)}, u32[]{:S(2)}) %collective-permute-start) | collective-permute-done | bytes 135200 | tf_op jit(solution)/shard_map/ppermute | solution.py:267
  10.9 0.9 fusion.9
  11.7 0.1 fusion.1
  11.8 0.9 fusion.13
  12.6 0.1 broadcast_bitcast_fusion.3
  12.7 1.1 %fusion.15 = bf16[512,128]{1,0:T(8,128)(2,1)S(1)} fusion(f32[512]{0:T(512)S(1)} %broadcast_bitcast_fusion.3, f32[528,128]{1,0:T(8,128)S(1)} %convert_element_type.84, f32[528,128]{1,0:T(8,128)} %get-tuple-element.17, pred[]{:T(512)S(6)} %eq.6), kind=kLoop, calls=%fused_computation.48 | loop fusion | flops 327680 | bytes 657409 | tf_op jit(solution)/shard_map/convert_element_type | solution.py:246
  13.8 0.2 maximum_maximum_fusion
  14.0 1.3 %collective-permute-start.1 = (bf16[528,128]{1,0:T(8,128)(2,1)S(1)}, bf16[528,128]{1,0:T(8,128)(2,1)S(1)}, u32[]{:S(2)}, u32[]{:S(2)}) collective-permute-start(bf16[528,128]{1,0:T(8,128)(2,1)S(1)} %maximum_maximum_fusion), channel_id=1, source_target_pairs={{0,8},{4,12},{8,16},{12,20},{16,24},{20,28},{1,9},{5,13},{9,17},{1... | collective-permute-start | bytes 405512 | tf_op jit(solution)/shard_map/ppermute | solution.py:284
  15.3 0.1 broadcast_bitcast_fusion
  15.4 0.1 broadcast_bitcast_fusion.2
  15.5 5.6 %collective-permute-done.1 = bf16[528,128]{1,0:T(8,128)(2,1)S(1)} collective-permute-done((bf16[528,128]{1,0:T(8,128)(2,1)S(1)}, bf16[528,128]{1,0:T(8,128)(2,1)S(1)}, u32[]{:S(2)}, u32[]{:S(2)}) %collective-permute-start.1) | collective-permute-done | bytes 135200 | tf_op jit(solution)/shard_map/ppermute | solution.py:284
  21.1 0.1 fusion.10
  21.2 0.1 fusion
  21.3 1.2 %add_convert_fusion.4 = bf16[512,128]{1,0:T(8,128)(2,1)S(1)} fusion(f32[528,128]{1,0:T(8,128)S(1)} %convert_element_type.88, f32[512]{0:T(512)S(1)} %broadcast_bitcast_fusion.2, f32[512]{0:T(512)S(1)} %broadcast_bitcast_fusion.3, f32[528,128]{1,0:T(8,128)S(1)} %convert_element_type.84, f32[528,128]{1,0:T(8,128)} %get-tuple-element.17, pred[]{:T(512)S(6)} %eq.6), kind=kLoop, calls=%fused_computation.9 | loop fusion | flops 458752 | bytes 921601 | tf_op jit(solution)/shard_map/convert_element_type | solution.py:246
  22.5 0.2 maximum_maximum_fusion.1
  22.7 1.3 %collective-permute-start.2 = (bf16[528,128]{1,0:T(8,128)(2,1)S(1)}, bf16[528,128]{1,0:T(8,128)(2,1)S(1)}, u32[]{:S(2)}, u32[]{:S(2)}) collective-permute-start(bf16[528,128]{1,0:T(8,128)(2,1)S(1)} %maximum_maximum_fusion.1), channel_id=1, source_target_pairs={{0,16},{4,20},{8,24},{12,28},{1,17},{5,21},{9,25},{13,29},{2,18},{... | collective-permute-start | bytes 405512 | tf_op jit(solution)/shard_map/ppermute | solution.py:284
  24.0 0.1 fusion.14
  24.1 0.1 broadcast_bitcast_fusion.1
  24.2 8.4 %collective-permute-done.2 = bf16[528,128]{1,0:T(8,128)(2,1)S(1)} collective-permute-done((bf16[528,128]{1,0:T(8,128)(2,1)S(1)}, bf16[528,128]{1,0:T(8,128)(2,1)S(1)}, u32[]{:S(2)}, u32[]{:S(2)}) %collective-permute-start.2) | collective-permute-done | bytes 135200 | tf_op jit(solution)/shard_map/ppermute | solution.py:284
  32.5 0.2 select_convert_fusion
  32.8 1.6 %collective-permute-start.3 = (bf16[512,128]{1,0:T(8,128)(2,1)S(1)}, bf16[512,128]{1,0:T(8,128)(2,1)S(1)}, u32[]{:S(2)}, u32[]{:S(2)}) collective-permute-start(bf16[512,128]{1,0:T(8,128)(2,1)S(1)} %select_convert_fusion), channel_id=1, source_target_pairs={{0,4},{4,0},{8,12},{12,8},{16,20},{20,16},{24,28},{28,24},{1,5},{5... | collective-permute-start | bytes 393224 | tf_op jit(solution)/shard_map/ppermute | solution.py:294
  34.3 0.7 copy.12
  35.0 4.0 %local.3.two_ref = f32[512,512]{1,0:T(8,128)} custom-call(f32[512,8]{1,0:T(8,128)} %get-tuple-element.16.cum_ref, f32[8,512]{1,0:T(8,128)} %bitcast.14, bf16[512,1024]{1,0:T(8,128)(2,1)} %q_ref.7, bf16[512,1024]{1,0:T(8,128)(2,1)} %key_ref.3, bf16[512,1024]{1,0:T(8,128)(2,1)} %value_ref.3), custom_call_target="tpu_custom_call" | custom-call | tf_op jit(solution)/shard_map/local/pallas_call | solution.py:135
  39.0 3.9 %local.2.one_ref = f32[512,512]{1,0:T(8,128)} custom-call(f32[512,8]{1,0:T(8,128)} %get-tuple-element.16.cum_ref, f32[8,512]{1,0:T(8,128)} %bitcast.15, bf16[512,1024]{1,0:T(8,128)(2,1)} %q_ref.7, bf16[512,1024]{1,0:T(8,128)(2,1)} %key_ref.3, bf16[512,1024]{1,0:T(8,128)(2,1)} %value_ref.3), custom_call_target="tpu_custom_call" | custom-call | tf_op jit(solution)/shard_map/local/pallas_call | solution.py:135
  42.9 0.6 pad_add_fusion.spot_ref
  43.5 0.0 collective-permute-done.3
  43.5 0.9 %broadcast_select_fusion = (bf16[512,128]{1,0:T(8,128)(2,1)}, bf16[512,128]{1,0:T(8,128)(2,1)S(1)}) fusion(bf16[512,128]{1,0:T(8,128)(2,1)S(1)} %collective-permute-done.3, pred[]{:T(512)S(6)} %eq.6, f32[528,128]{1,0:T(8,128)S(1)} %convert_element_type.84, f32[528,128]{1,0:T(8,128)S(1)} %copy-done.2, f32[512]{0:T(512)S(1)} %broadcast_bitcast_fusion, ...), kind=kLoop, calls=%fused_computation.14 | loop fusion | flops 589824 | bytes 1314817 | tf_op jit(solution)/shard_map/jit(_where)/select_n | solution.py:296
  44.4 0.7 broadcast_select_fusion.1.low_ref
  45.1 4.3 %norm_away.1 = bf16[256,1024]{1,0:T(8,128)(2,1)} custom-call(s32[2]{0:T(128)} %pad_add_fusion.spot_ref, f32[512,8]{1,0:T(8,128)} %get-tuple-element.16.cum_ref, bf16[512,1024]{1,0:T(8,128)(2,1)} %q_ref.7, f32[512,512]{1,0:T(8,128)} %local.2.one_ref, f32[512,512]{1,0:T(8,128)} %local.3.two_ref, bf16[512,128]{1,0:T(8,128)(2,1)} %broadcast_select_fusion.1.low_ref, ...), custom_call_target="tpu_custom_call" | custom-call | tf_op jit(solution)/shard_map/norm_away/pallas_call | solution.py:174
  49.4 4.3 %norm_home.1.mine_ref = bf16[256,1024]{1,0:T(8,128)(2,1)} custom-call(s32[2]{0:T(128)} %pad_add_fusion.spot_ref, f32[512,8]{1,0:T(8,128)} %get-tuple-element.16.cum_ref, bf16[512,1024]{1,0:T(8,128)(2,1)} %q_ref.7, f32[512,512]{1,0:T(8,128)} %local.2.one_ref, f32[512,512]{1,0:T(8,128)} %local.3.two_ref, bf16[512,128]{1,0:T(8,128)(2,1)} %broadcast_select_fusion.1.low_ref, ...), custom_call_target="tpu_custom_call" | custom-call | tf_op jit(solution)/shard_map/norm_home/pallas_call | solution.py:174
  53.7 0.8 copy-done
  54.5 4.1 %project.6 = (f32[128,1024]{1,0:T(8,128)}, bf16[128,1024]{1,0:T(8,128)(2,1)}) custom-call(bf16[256,1024]{1,0:T(8,128)(2,1)} %norm_home.1.mine_ref, bf16[256,1024]{1,0:T(8,128)(2,1)} %copy-done, bf16[1024,4096]{1,0:T(8,128)(2,1)} %near_ref.7, bf16[1024,4096]{1,0:T(8,128)(2,1)} %collective-permute-done.5.far_ref), custom_call_target="tpu_custom_call" | custom-call | tf_op jit(solution)/shard_map/project/pallas_call | solution.py:206
  58.6 1.5 %collective-permute-start.8 = (bf16[128,1024]{1,0:T(8,128)(2,1)}, bf16[128,1024]{1,0:T(8,128)(2,1)S(1)}, u32[]{:S(2)}, u32[]{:S(2)}) collective-permute-start(bf16[128,1024]{1,0:T(8,128)(2,1)} %get-tuple-element.24), channel_id=1, source_target_pairs={{0,2},{1,3},{2,0},{3,1},{4,6},{5,7},{6,4},{7,5},{8,10},{9,11},{10,... | collective-permute-start | bytes 786440 | tf_op jit(solution)/shard_map/ppermute | solution.py:315
  60.1 4.1 %project.7 = (f32[128,1024]{1,0:T(8,128)}, bf16[128,1024]{1,0:T(8,128)(2,1)}) custom-call(bf16[256,1024]{1,0:T(8,128)(2,1)} %norm_home.1.mine_ref, bf16[256,1024]{1,0:T(8,128)(2,1)} %copy-done, bf16[1024,4096]{1,0:T(8,128)(2,1)} %near_ref.7, bf16[1024,4096]{1,0:T(8,128)(2,1)} %collective-permute-done.5.far_ref), custom_call_target="tpu_custom_call" | custom-call | tf_op jit(solution)/shard_map/project/pallas_call | solution.py:206
  64.2 0.5 collective-permute-start.9
  64.7 4.0 %project.5 = (f32[128,1024]{1,0:T(8,128)}, bf16[128,1024]{1,0:T(8,128)(2,1)}) custom-call(bf16[256,1024]{1,0:T(8,128)(2,1)} %norm_home.1.mine_ref, bf16[256,1024]{1,0:T(8,128)(2,1)} %copy-done, bf16[1024,4096]{1,0:T(8,128)(2,1)} %near_ref.7, bf16[1024,4096]{1,0:T(8,128)(2,1)} %collective-permute-done.5.far_ref), custom_call_target="tpu_custom_call" | custom-call | tf_op jit(solution)/shard_map/project/pallas_call | solution.py:206
  68.7 1.6 %collective-permute-start.7 = (bf16[128,1024]{1,0:T(8,128)(2,1)}, bf16[128,1024]{1,0:T(8,128)(2,1)S(1)}, u32[]{:S(2)}, u32[]{:S(2)}) collective-permute-start(bf16[128,1024]{1,0:T(8,128)(2,1)} %get-tuple-element.22), channel_id=1, source_target_pairs={{0,2},{1,3},{2,0},{3,1},{4,6},{5,7},{6,4},{7,5},{8,10},{9,11},{10,... | collective-permute-start | bytes 786440 | tf_op jit(solution)/shard_map/ppermute | solution.py:315
  70.3 4.0 %project.4 = (f32[128,1024]{1,0:T(8,128)}, bf16[128,1024]{1,0:T(8,128)(2,1)}) custom-call(bf16[256,1024]{1,0:T(8,128)(2,1)} %norm_home.1.mine_ref, bf16[256,1024]{1,0:T(8,128)(2,1)} %copy-done, bf16[1024,4096]{1,0:T(8,128)(2,1)} %near_ref.7, bf16[1024,4096]{1,0:T(8,128)(2,1)} %collective-permute-done.5.far_ref), custom_call_target="tpu_custom_call" | custom-call | tf_op jit(solution)/shard_map/project/pallas_call | solution.py:206
  74.3 0.7 collective-permute-start.6
  75.0 4.2 %collective-permute-done.7 = bf16[128,1024]{1,0:T(8,128)(2,1)S(1)} collective-permute-done((bf16[128,1024]{1,0:T(8,128)(2,1)}, bf16[128,1024]{1,0:T(8,128)(2,1)S(1)}, u32[]{:S(2)}, u32[]{:S(2)}) %collective-permute-start.7) | collective-permute-done | bytes 262176 | tf_op jit(solution)/shard_map/ppermute | solution.py:315
  79.2 5.2 %collective-permute-done.6 = bf16[128,1024]{1,0:T(8,128)(2,1)S(1)} collective-permute-done((bf16[128,1024]{1,0:T(8,128)(2,1)}, bf16[128,1024]{1,0:T(8,128)(2,1)S(1)}, u32[]{:S(2)}, u32[]{:S(2)}) %collective-permute-start.6) | collective-permute-done | bytes 262176 | tf_op jit(solution)/shard_map/ppermute | solution.py:315
  84.4 1.6 %add_convert_fusion.3 = (bf16[128,1024]{1,0:T(8,128)(2,1)S(1)}, bf16[128,1024]{1,0:T(8,128)(2,1)S(1)}, bf16[128,1024]{1,0:T(8,128)(2,1)S(1)}, bf16[128,1024]{1,0:T(8,128)(2,1)S(1)}) fusion(bf16[128,1024]{1,0:T(8,128)(2,1)S(1)} %collective-permute-done.6, f32[128,1024]{1,0:T(8,128)} %get-tuple-element.19, bf16[128,4096]{1,0:T(8,128)(2,1)S(1)} %copy-done.3, ...), kind=kLoop, calls=%fused_computation.4 | loop fusion | flops 2621440 | bytes 5242880 | tf_op jit(solution)/shard_map/convert_element_type | solution.py:316
  86.0 1.0 %pad_maximum_fusion = bf16[128,4096]{1,0:T(8,128)(2,1)} fusion(bf16[128,1024]{1,0:T(8,128)(2,1)S(1)} %get-tuple-element.38, bf16[128,1024]{1,0:T(8,128)(2,1)S(1)} %get-tuple-element.39, bf16[128,1024]{1,0:T(8,128)(2,1)S(1)} %get-tuple-element.37, bf16[128,1024]{1,0:T(8,128)(2,1)S(1)} %get-tuple-element.36), kind=kLoop, calls=%fused_computation | loop fusion | flops 4194304 | bytes 2097152 | tf_op jit(solution)/shard_map/concatenate | solution.py:317
  (22 shorter events, 0.1 us)
Async XLA Ops:
  0.0 53.7 %collective-permute-start.5 = (bf16[1024,4096]{1,0:T(8,128)(2,1)}, bf16[1024,4096]{1,0:T(8,128)(2,1)}, u32[]{:S(2)}, u32[]{:S(2)}) collective-permute-start(bf16[1024,4096]{1,0:T(8,128)(2,1)} %near_ref.7), channel_id=1, source_target_pairs={{0,1},{1,0},{2,3},{3,2},{4,5},{5,4},{6,7},{7,6},{8,9},{9,8},{10,11... | collective-permute-start | bytes 25165832 | tf_op jit(solution)/shard_map/ppermute | solution.py:268
  4.6 6.2 %collective-permute-start = (bf16[528,128]{1,0:T(8,128)(2,1)}, bf16[528,128]{1,0:T(8,128)(2,1)S(1)}, u32[]{:S(2)}, u32[]{:S(2)}) collective-permute-start(bf16[528,128]{1,0:T(8,128)(2,1)} %get-tuple-element.18), channel_id=1, source_target_pairs={{0,4},{4,0},{8,12},{12,8},{16,20},{20,16},{24,28},{28,24},{1,5},{5... | collective-permute-start | bytes 405512 | tf_op jit(solution)/shard_map/ppermute | solution.py:267
  9.2 23.4 %copy-start.2 = (f32[528,128]{1,0:T(8,128)S(1)}, f32[528,128]{1,0:T(8,128)}, u32[]{:S(2)}) copy-start(f32[528,128]{1,0:T(8,128)} %get-tuple-element.17) | copy-start | bytes 811012
  9.2 25.1 %copy-start.1 = (f32[512,8]{1,0:T(8,128)S(1)}, f32[512,8]{1,0:T(8,128)}, u32[]{:S(2)}) copy-start(f32[512,8]{1,0:T(8,128)} %get-tuple-element.16.cum_ref) | copy-start | bytes 49156
  14.0 7.0 %collective-permute-start.1 = (bf16[528,128]{1,0:T(8,128)(2,1)S(1)}, bf16[528,128]{1,0:T(8,128)(2,1)S(1)}, u32[]{:S(2)}, u32[]{:S(2)}) collective-permute-start(bf16[528,128]{1,0:T(8,128)(2,1)S(1)} %maximum_maximum_fusion), channel_id=1, source_target_pairs={{0,8},{4,12},{8,16},{12,20},{16,24},{20,28},{1,9},{5,13},{9,17},{1... | collective-permute-start | bytes 405512 | tf_op jit(solution)/shard_map/ppermute | solution.py:284
  22.7 9.8 %collective-permute-start.2 = (bf16[528,128]{1,0:T(8,128)(2,1)S(1)}, bf16[528,128]{1,0:T(8,128)(2,1)S(1)}, u32[]{:S(2)}, u32[]{:S(2)}) collective-permute-start(bf16[528,128]{1,0:T(8,128)(2,1)S(1)} %maximum_maximum_fusion.1), channel_id=1, source_target_pairs={{0,16},{4,20},{8,24},{12,28},{1,17},{5,21},{9,25},{13,29},{2,18},{... | collective-permute-start | bytes 405512 | tf_op jit(solution)/shard_map/ppermute | solution.py:284
  32.8 10.7 %collective-permute-start.3 = (bf16[512,128]{1,0:T(8,128)(2,1)S(1)}, bf16[512,128]{1,0:T(8,128)(2,1)S(1)}, u32[]{:S(2)}, u32[]{:S(2)}) collective-permute-start(bf16[512,128]{1,0:T(8,128)(2,1)S(1)} %select_convert_fusion), channel_id=1, source_target_pairs={{0,4},{4,0},{8,12},{12,8},{16,20},{20,16},{24,28},{28,24},{1,5},{5... | collective-permute-start | bytes 393224 | tf_op jit(solution)/shard_map/ppermute | solution.py:294
  49.4 4.3 %collective-permute-start.4 = (bf16[256,1024]{1,0:T(8,128)(2,1)}, bf16[256,1024]{1,0:T(8,128)(2,1)S(1)}, u32[]{:S(2)}, u32[]{:S(2)}) collective-permute-start(bf16[256,1024]{1,0:T(8,128)(2,1)} %norm_away.1), channel_id=1, source_target_pairs={{0,1},{1,0},{2,3},{3,2},{4,5},{5,4},{6,7},{7,6},{8,9},{9,8},{10,11... | collective-permute-start | bytes 1572872 | tf_op jit(solution)/shard_map/ppermute | solution.py:302
  53.7 0.8 copy-start
  58.6 16.4 %collective-permute-start.8 = (bf16[128,1024]{1,0:T(8,128)(2,1)}, bf16[128,1024]{1,0:T(8,128)(2,1)S(1)}, u32[]{:S(2)}, u32[]{:S(2)}) collective-permute-start(bf16[128,1024]{1,0:T(8,128)(2,1)} %get-tuple-element.24), channel_id=1, source_target_pairs={{0,2},{1,3},{2,0},{3,1},{4,6},{5,7},{6,4},{7,5},{8,10},{9,11},{10,... | collective-permute-start | bytes 786440 | tf_op jit(solution)/shard_map/ppermute | solution.py:315
  64.2 10.8 %collective-permute-start.9 = (bf16[128,1024]{1,0:T(8,128)(2,1)}, bf16[128,1024]{1,0:T(8,128)(2,1)S(1)}, u32[]{:S(2)}, u32[]{:S(2)}) collective-permute-start(bf16[128,1024]{1,0:T(8,128)(2,1)} %get-tuple-element.26), channel_id=1, source_target_pairs={{0,2},{1,3},{2,0},{3,1},{4,6},{5,7},{6,4},{7,5},{8,10},{9,11},{10,... | collective-permute-start | bytes 786440 | tf_op jit(solution)/shard_map/ppermute | solution.py:315
  68.7 15.7 %copy-start.3 = (bf16[128,4096]{1,0:T(8,128)(2,1)S(1)}, bf16[128,4096]{1,0:T(8,128)(2,1)}, u32[]{:S(2)}) copy-start(bf16[128,4096]{1,0:T(8,128)(2,1)} %param.13) | copy-start | bytes 3145732
  68.7 15.7 %copy-start.4 = (f32[128,1024]{1,0:T(8,128)S(1)}, f32[128,1024]{1,0:T(8,128)}, u32[]{:S(2)}) copy-start(f32[128,1024]{1,0:T(8,128)} %get-tuple-element.23) | copy-start | bytes 1572868
  68.7 15.7 %copy-start.5 = (f32[128,1024]{1,0:T(8,128)S(1)}, f32[128,1024]{1,0:T(8,128)}, u32[]{:S(2)}) copy-start(f32[128,1024]{1,0:T(8,128)} %get-tuple-element.25) | copy-start | bytes 1572868
  68.7 15.7 %copy-start.6 = (f32[128,1024]{1,0:T(8,128)S(1)}, f32[128,1024]{1,0:T(8,128)}, u32[]{:S(2)}) copy-start(f32[128,1024]{1,0:T(8,128)} %get-tuple-element.21) | copy-start | bytes 1572868
  68.7 10.5 %collective-permute-start.7 = (bf16[128,1024]{1,0:T(8,128)(2,1)}, bf16[128,1024]{1,0:T(8,128)(2,1)S(1)}, u32[]{:S(2)}, u32[]{:S(2)}) collective-permute-start(bf16[128,1024]{1,0:T(8,128)(2,1)} %get-tuple-element.22), channel_id=1, source_target_pairs={{0,2},{1,3},{2,0},{3,1},{4,6},{5,7},{6,4},{7,5},{8,10},{9,11},{10,... | collective-permute-start | bytes 786440 | tf_op jit(solution)/shard_map/ppermute | solution.py:315
  74.3 10.0 %collective-permute-start.6 = (bf16[128,1024]{1,0:T(8,128)(2,1)}, bf16[128,1024]{1,0:T(8,128)(2,1)S(1)}, u32[]{:S(2)}, u32[]{:S(2)}) collective-permute-start(bf16[128,1024]{1,0:T(8,128)(2,1)} %get-tuple-element.20), channel_id=1, source_target_pairs={{0,2},{1,3},{2,0},{3,1},{4,6},{5,7},{6,4},{7,5},{8,10},{9,11},{10,... | collective-permute-start | bytes 786440 | tf_op jit(solution)/shard_map/ppermute | solution.py:315

commit v2 on v0

v2 whole, which is shorter than its diff:
```python
import functools

import jax
import jax.numpy as jnp
from jax import lax
from jax.experimental import pallas as pl
from jax.experimental.pallas import tpu as pltpu
from jax.sharding import PartitionSpec as P

F32 = jnp.float32
BF16 = jnp.bfloat16
PARAMS = pltpu.CompilerParams(vmem_limit_bytes=16 << 20)
VMEM = pl.BlockSpec(memory_space=pltpu.VMEM)
SMEM = pl.BlockSpec(memory_space=pltpu.SMEM)
ANY = pl.BlockSpec(memory_space=pl.ANY)


def held(shape, kind):
    return pltpu.VMEM(shape, kind)


def near(x):
    return pltpu.with_memory_space_constraint(x, pltpu.VMEM)


def outside(x):
    return pltpu.with_memory_space_constraint(x, pltpu.HBM)


def tile_of(size, want):
    while size % want:
        want //= 2
    return want


def pad_rows(count):
    return -(-count // 8) * 8


def running_sum(logd):
    heads, rows = logd.shape
    tile = tile_of(rows, 128)
    count = rows // tile
    tiles = jnp.concatenate([logd[:, i * tile : (i + 1) * tile] for i in range(count)], axis=0)
    one = tiles.astype(BF16).astype(F32)
    two = (tiles - one).astype(BF16).astype(F32)
    three = tiles - one - two
    parts = jnp.concatenate([one, two, three], axis=0).astype(BF16)
    upper = (
        lax.broadcasted_iota(jnp.int32, (tile, tile), 0)
        <= lax.broadcasted_iota(jnp.int32, (tile, tile), 1)
    ).astype(F32)
    sums = jnp.dot(parts, upper.astype(BF16), preferred_element_type=F32)
    size = count * heads
    sums = sums[:size] + sums[size : 2 * size] + sums[2 * size :]
    done, carry = [], None
    for i in range(count):
        part = sums[i * heads : (i + 1) * heads]
        if carry is not None:
            part = part + carry
        carry = part[:, tile - 1 : tile]
        done.append(part)
    return jnp.concatenate(done, axis=1)


def state_kernel(half, width, which_ref, logd_ref, key_ref, value_ref, pay_ref, cum_ref):
    second = which_ref[0] == 1
    cum = running_sum(logd_ref[...])
    cum_ref[...] = cum
    rows = cum.shape[1]
    totals = cum[:, rows - 1 : rows]
    weights = jnp.exp(totals - cum)
    narrow = pay_ref.dtype == BF16
    pad = pad_rows(half)
    base = half * width
    highs, lows = [], []
    for j in range(half):
        weight = jnp.where(second, weights[half + j : half + j + 1], weights[j : j + 1])
        total = jnp.where(second, totals[half + j : half + j + 1], totals[j : j + 1])
        cols = slice(j * width, (j + 1) * width)
        keyed = (key_ref[:, cols].T.astype(F32) * weight).astype(BF16)
        state = jnp.dot(keyed, value_ref[:, cols], preferred_element_type=F32)
        pay_ref[j * width : (j + 1) * width, :] = state.astype(pay_ref.dtype)
        decay = jnp.broadcast_to(jnp.exp(total), (1, width))
        if narrow:
            high = decay.astype(BF16).astype(F32)
            highs.append(high)
            lows.append(decay - high)
        else:
            highs.append(decay)
            lows.append(jnp.zeros_like(decay))
    blank = [jnp.zeros((1, width), F32)] * (pad - half)
    tail = jnp.concatenate(highs + blank + lows + blank, axis=0)
    pay_ref[base:, :] = tail.astype(pay_ref.dtype)


def states(which, logd, key, value, half, width, kind):
    heads, rows = logd.shape
    cols = half * width
    tall = cols + 2 * pad_rows(half)
    return pl.pallas_call(
        functools.partial(state_kernel, half, width),
        grid_spec=pltpu.PrefetchScalarGridSpec(
            num_scalar_prefetch=1,
            grid=(1,),
            in_specs=[
                pl.BlockSpec((heads, rows), lambda i, w: (0, 0)),
                pl.BlockSpec((rows, cols), lambda i, w: (0, w[0])),
                pl.BlockSpec((rows, cols), lambda i, w: (0, w[0])),
            ],
            out_specs=[VMEM, VMEM],
        ),
        out_shape=[
            held((tall, width), kind),
            held((heads, rows), F32),
        ],
        compiler_params=PARAMS,
        name="states",
    )(which, logd, outside(key), outside(value))


def decay_row(pay, j, half, width):
    at = half * width + j
    pad = pad_rows(half)
    return pay[at : at + 1, :].astype(F32) + pay[at + pad : at + pad + 1, :].astype(F32)


def put_decays(ref, rows, half, width):
    pad = pad_rows(half)
    blank = [jnp.zeros((1, width), F32)] * (pad - half)
    if ref.dtype == BF16:
        highs = [row.astype(BF16).astype(F32) for row in rows]
        lows = [row - high for row, high in zip(rows, highs)]
    else:
        highs, lows = rows, [jnp.zeros_like(row) for row in rows]
    tail = jnp.concatenate(highs + blank + lows + blank, axis=0)
    ref[half * width :, :] = tail.astype(ref.dtype)


def pair_kernel(half, width, side_ref, own_ref, met_ref, pay_ref, window_ref, first_ref):
    is_first = side_ref[0] == 0
    decays, firsts = [], []
    for j in range(half):
        rows = slice(j * width, (j + 1) * width)
        own, met = own_ref[rows, :], met_ref[rows, :].astype(F32)
        own_decay = decay_row(own_ref, j, half, width)
        met_decay = decay_row(met_ref, j, half, width)
        first = jnp.where(is_first, own, met)
        second = jnp.where(is_first, met, own)
        window = first * jnp.where(is_first, met_decay, own_decay) + second
        window_ref[rows, :] = window
        pay_ref[rows, :] = window.astype(pay_ref.dtype)
        first_ref[rows, :] = first
        decays.append(own_decay * met_decay)
        firsts.append(jnp.where(is_first, own_decay, met_decay))
    put_decays(pay_ref, decays, half, width)
    put_decays(window_ref, decays, half, width)
    put_decays(first_ref, firsts, half, width)


def pair(side, own, met, half, width):
    shape = own.shape
    return pl.pallas_call(
        functools.partial(pair_kernel, half, width),
        in_specs=[SMEM, VMEM, VMEM],
        out_specs=[VMEM, VMEM, VMEM],
        out_shape=[
            held(shape, BF16),
            held(shape, F32),
            held(shape, F32),
        ],
        compiler_params=PARAMS,
        name="pair",
    )(side, near(own), near(met))


def widen_kernel(half, width, opening, got_ref, window_ref, before_ref, hold_ref, pay_ref, wide_ref, past_ref):
    decays, pasts = [], []
    for j in range(half):
        rows = slice(j * width, (j + 1) * width)
        got = got_ref[rows, :].astype(F32)
        got_decay = decay_row(got_ref, j, half, width)
        window_decay = decay_row(window_ref, j, half, width)
        wide = got * window_decay + window_ref[rows, :]
        wide_ref[rows, :] = wide
        pay_ref[rows, :] = wide.astype(pay_ref.dtype)
        decays.append(got_decay * window_decay)
        if opening:
            past_ref[rows, :] = got
            pasts.append(got_decay)
        else:
            before_decay = decay_row(before_ref, j, half, width)
            past_ref[rows, :] = got * before_decay + before_ref[rows, :]
            pasts.append(got_decay * before_decay)
    put_decays(pay_ref, decays, half, width)
    put_decays(wide_ref, decays, half, width)
    put_decays(past_ref, pasts, half, width)


def widen(got, window, before, hold, half, width):
    shape = window.shape
    opening = before is None
    return pl.pallas_call(
        functools.partial(widen_kernel, half, width, opening),
        in_specs=[VMEM, VMEM, VMEM, ANY],
        out_specs=[VMEM, VMEM, VMEM],
        out_shape=[
            held(shape, BF16),
            held(shape, F32),
            held(shape, F32),
        ],
        compiler_params=PARAMS,
        name="widen",
    )(near(got), near(window), near(window if opening else before), hold)


def enter_kernel(half, width, rounds, side_ref, got_ref, before_ref, first_ref, hold_ref, mine_ref, theirs_ref):
    is_first = side_ref[0] == 0
    for j in range(half):
        rows = slice(j * width, (j + 1) * width)
        if rounds == 0:
            before = jnp.zeros((width, width), F32)
        else:
            before = got_ref[rows, :].astype(F32)
            if rounds > 1:
                before = before * decay_row(before_ref, j, half, width) + before_ref[rows, :]
        after = before * decay_row(first_ref, j, half, width) + first_ref[rows, :]
        mine_ref[rows, :] = jnp.where(is_first, before, after).astype(BF16)
        theirs_ref[rows, :] = jnp.where(is_first, after, before).astype(BF16)


def enter(side, got, before, first, hold, half, width, rounds):
    shape = (half * width, width)
    got = first if got is None else got
    before = first if before is None else before
    return pl.pallas_call(
        functools.partial(enter_kernel, half, width, rounds),
        in_specs=[SMEM, VMEM, VMEM, VMEM, ANY],
        out_specs=[VMEM, VMEM],
        out_shape=[held(shape, BF16)] * 2,
        compiler_params=PARAMS,
        name="enter",
    )(side, near(got), near(before), near(first), hold)


def local_kernel(heads, width, cum_ref, q_ref, k_ref, v_ref, hold_ref, out_ref, decayed_ref):
    rows = cum_ref.shape[1]
    tile = tile_of(rows, width)
    causal = lax.broadcasted_iota(jnp.int32, (tile, tile), 0) >= lax.broadcasted_iota(
        jnp.int32, (tile, tile), 1
    )
    for j, head in enumerate(heads):
        cols = slice(j * width, (j + 1) * width)
        cum = cum_ref[head : head + 1, :]
        for i in range(rows // tile):
            here = slice(i * tile, (i + 1) * tile)
            query = q_ref[here, cols]
            across = jnp.broadcast_to(cum[:, here], (tile, tile))
            down = across.T
            scores = lax.dot_general(
                query, k_ref[here, cols], (((1,), (1,)), ((), ())), preferred_element_type=F32
            )
            weight = jnp.exp(jnp.where(causal, down - across, -jnp.inf))
            out = jnp.dot(
                (scores * weight).astype(BF16), v_ref[here, cols], preferred_element_type=F32
            )
            if i == 0:
                decay = jnp.exp(down)
            else:
                edge = cum[:, i * tile - 1 : i * tile]
                since = jnp.exp(down - edge)
                earlier = slice(0, i * tile)
                scores = lax.dot_general(
                    query, k_ref[earlier, cols], (((1,), (1,)), ((), ())), preferred_element_type=F32
                )
                weight = jnp.exp(edge - cum[:, earlier])
                out = out + since[:, :1] * jnp.dot(
                    (scores * weight).astype(BF16), v_ref[earlier, cols], preferred_element_type=F32
                ) if tile != width else out + since * jnp.dot(
                    (scores * weight).astype(BF16), v_ref[earlier, cols], preferred_element_type=F32
                )
                decay = since * jnp.exp(edge)
            out_ref[here, cols] = out
            decay = decay if tile == width else decay[:, :1]
            decayed_ref[here, cols] = (query.astype(F32) * decay).astype(BF16)


def local(cum, query, key, value, hold, part, parts, heads, width):
    rows = cum.shape[1]
    count = heads // parts
    cols = count * width
    block = pl.BlockSpec((rows, cols), lambda i: (0, part))
    return pl.pallas_call(
        functools.partial(local_kernel, tuple(range(part * count, (part + 1) * count)), width),
        grid=(1,),
        in_specs=[VMEM, block, block, block, ANY],
        out_specs=[VMEM, VMEM],
        out_shape=[
            held((rows, cols), F32),
            held((rows, cols), BF16),
        ],
        compiler_params=PARAMS,
        name="local",
    )(near(cum), outside(query), outside(key), outside(value), hold)


def norm_kernel(half, width, parts, chips, block, away, spot_ref, mine_ref, met_ref, gain_ref, *refs):
    inside_refs, query_refs, out_ref = refs[:parts], refs[parts : 2 * parts], refs[-1]
    per = 2 * half // parts
    is_first = spot_ref[2] == 0
    ones = jnp.full((width, width), 1.0 / width, F32).astype(BF16)
    for head in range(2 * half):
        span = slice((head % half) * width, (head % half + 1) * width)
        is_mine = is_first if head < half else jnp.logical_not(is_first)
        state = jnp.where(is_mine, mine_ref[span, :], met_ref[span, :])
        inside_ref, query_ref = inside_refs[head // per], query_refs[head // per]
        src = slice((head % per) * width, (head % per + 1) * width)
        cols = slice(head * width, (head + 1) * width)
        gain = gain_ref[:, cols]
        for i in range(chips):
            at = 2 * lax.rem(spot_ref[0] + i, chips)
            at = at + (1 - spot_ref[1] if away else spot_ref[1])
            rows = pl.ds(pl.multiple_of(at * block, block), block)
            attended = inside_ref[rows, src] + jnp.dot(
                query_ref[rows, src], state, preferred_element_type=F32
            )
            square = jnp.dot(
                (attended * attended).astype(BF16), ones, preferred_element_type=F32
            )
            out_ref[i * block : (i + 1) * block, cols] = (
                attended * lax.rsqrt(square + 1e-06) * gain
            ).astype(out_ref.dtype)


def norm(spot, mine, met, gain, insides, queries, half, width, chips, block, away):
    parts = len(insides)
    return pl.pallas_call(
        functools.partial(norm_kernel, half, width, parts, chips, block, away),
        in_specs=[SMEM] + [VMEM] * (3 + 2 * parts),
        out_specs=VMEM,
        out_shape=held((chips * block, 2 * half * width), BF16),
        compiler_params=PARAMS,
        name="norm_away" if away else "norm_home",
    )(spot, near(mine), near(met), gain, *map(near, insides), *map(near, queries))


def project_kernel(block, first, tile, mine_ref, other_ref, near_ref, far_ref, own_ref, away_ref):
    for i in range(own_ref.shape[1] // tile):
        cols = slice(first + i * tile, first + (i + 1) * tile)
        total = jnp.dot(mine_ref[...], near_ref[:, cols], preferred_element_type=F32) + jnp.dot(
            other_ref[...], far_ref[:, cols], preferred_element_type=F32
        )
        span = slice(i * tile, (i + 1) * tile)
        own_ref[:, span] = total[:block]
        away_ref[:, span] = total[block:].astype(away_ref.dtype)


def project(mine, other, first_weight, second_weight, block, first, count, tile):
    rows, depth = mine.shape
    return pl.pallas_call(
        functools.partial(project_kernel, block, first, tile),
        in_specs=[
            VMEM,
            VMEM,
            VMEM,
            VMEM,
        ],
        out_specs=[VMEM, VMEM],
        out_shape=[
            held((block, count), F32),
            held((rows - block, count), BF16),
        ],
        compiler_params=PARAMS,
        name="project",
    )(near(mine), near(other), near(first_weight), near(second_weight))


def shards(blocks, group, q_spikes, k_spikes, v_spikes, log_decay, norm_gain, out_weight, residual):
    rows, heads = log_decay.shape
    width = q_spikes.shape[1] // heads
    half = heads // 2
    chips = group // 2
    block = rows // group
    parts = min(4, heads)
    place = lax.axis_index("ctx")
    member = lax.axis_index("exp")
    side = (place & 1).astype(jnp.int32)
    swap = [(i, i ^ 1) for i in range(blocks)]
    cores = [(i, i ^ 1) for i in range(group)]

    logd = log_decay.T
    if heads % 8:
        logd = jnp.pad(logd, ((0, pad_rows(heads) - heads), (0, 0)))
    sent, _ = states((1 - side).reshape(1), logd, k_spikes, v_spikes, half, width, BF16)
    met = lax.ppermute(sent, "ctx", swap)
    far_weight = lax.ppermute(out_weight, "exp", cores)
    side = side.reshape(1)
    kept, cum = states(side, logd, k_spikes, v_spikes, half, width, F32)

    inner = []

    def more(hold):
        if len(inner) < parts:
            inner.append(
                local(cum, q_spikes, k_spikes, v_spikes, hold, len(inner), parts, heads, width)
            )
        return inner[-1][0]

    pay, window, first = pair(side, kept, met, half, width)
    before, got, rounds, step = None, None, 0, 1
    hold = pay
    while 2 * step < blocks:
        got = lax.ppermute(pay, "ctx", [(i, i + 2 * step) for i in range(blocks - 2 * step)])
        hold = more(pay)
        rounds += 1
        step *= 2
        if 2 * step < blocks:
            pay, window, before = widen(got, window, before, hold, half, width)
    mine, theirs = enter(side, got, before, first, hold, half, width, rounds)
    met = lax.ppermute(theirs, "ctx", swap)
    while len(inner) < parts:
        more(theirs)

    spot = jnp.stack([member >> 1, member & 1, place & 1]).astype(jnp.int32)
    gain = norm_gain.reshape(1, heads * width)
    insides, queries = [a for a, _ in inner], [b for _, b in inner]
    args = (spot, mine, met, gain, insides, queries, half, width, chips, block)
    away = norm(*args, True)
    other = lax.ppermute(away, "exp", cores)
    home = norm(*args, False)

    total = out_weight.shape[1]
    tile = tile_of(total, 512)
    sizes = [tile]
    while sum(sizes) < total:
        sizes.append(min(2 * tile, max(tile, total - sum(sizes) - tile)))
    out = jnp.zeros((block, total), BF16)
    at = 0
    for size in sizes:
        own, pieces = project(home, other, out_weight, far_weight, block, at, size, tile)
        summed = own + residual[:, at : at + size].astype(F32)
        for d in range(1, chips):
            piece = pieces[(d - 1) * block : d * block]
            perm = [(i, 2 * ((i // 2 + d) % chips) + i % 2) for i in range(group)]
            summed = summed + lax.ppermute(piece, "exp", perm).astype(F32)
        out = lax.dynamic_update_slice(out, summed.astype(BF16), (0, at))
        at += size
    return out


def solution(mesh):
    in_specs = (
        P("ctx", "exp"),
        P("ctx", "exp"),
        P("ctx", "exp"),
        P("ctx", "exp"),
        P("exp"),
        P("exp", None),
        P(("ctx", "exp"), None),
    )
    out_specs = P(("ctx", "exp"), None)
    return jax.shard_map(
        functools.partial(shards, mesh.shape["ctx"], mesh.shape["exp"]),
        mesh=mesh,
        in_specs=in_specs,
        out_specs=out_specs,
        check_vma=False,
    )
```

time: 140 us -> 73.5 us (0.53); the launches traced: 138 us -> 72.9 us
  waiting for transfers between devices: 70.7 us -> 16 us
  Pallas kernels: 0 us -> 39 us
  matrix products: 23.3 us -> 0 us
  blocking collectives: 15.9 us -> 0 us
  between operations: 13.5 us -> 0.23 us
  starting transfers between devices: 0.04 us -> 11.6 us
  other arithmetic: 12.1 us -> 1.07 us
  local copies, waits for them, and re-layouts: 2.09 us -> 4.93 us
    reduce_scatter x1 -> x0, waiting for transfers between devices: 45.9 us -> none  [shards(): lax.psum_scatter(jnp.dot(normed, out_weight, preferred_element_type=jnp.f...]
    pallas_call x0 -> x16, Pallas kernels: none -> 39 us  [the longest x5 22 us: project(): pl.pallas_call(functools.partial(project_kernel, block, first, tile), in_...]
    all_gather x1 -> x0, waiting for transfers between devices: 24.8 us -> none  [entering(): lax.all_gather(a.astype(kind), axis)]
    dot_general x5 -> x0, matrix products: 23.3 us -> none  [the longest x1 9.48 us: shards(): jnp.dot(normed, out_weight, preferred_element_type=jnp.float32)]
    ppermute x0 -> x11, waiting for transfers between devices: none -> 16 us  [the longest x2 9.35 us: shards(): lax.ppermute(pay, 'ctx', [(i, i + 2 * step) for i in range(blocks - 2 * s...]
    all_gather x1 -> x0, blocking collectives: 15.9 us -> none  [entering(): lax.all_gather(a.astype(kind), axis)]
    ppermute x0 -> x11, starting transfers between devices: none -> 11.6 us  [the longest x5 5.9 us: shards(): summed = summed + lax.ppermute(piece, 'exp', perm).astype(F32)]
    add x6 -> x0, other arithmetic: 6.66 us -> none  [combine(): earlier[1] * jnp.exp(later[0])[:, None, None] + later[1]]
  transfers between devices with their start and end apart: 2 -> 11, of which waited for: 2 -> 6; matrix products, arithmetic and copies ran while one was open for 6% -> 1% of each run, Pallas kernels for 0% -> 48%
where the time goes in v2:
time: 73.5 us; the launch traced here: 72.9 us
  Pallas kernels  39 us (53%)
  waiting for transfers between devices  16 us (22%)
  starting transfers between devices  11.6 us (16%)
  local copies, waits for them, and re-layouts  4.93 us (7%)
  other arithmetic  1.07 us (1%)
    pallas_call x5, Pallas kernels, project(): pl.pallas_call(functools.partial(project_kernel, block, first, tile), in_...  22 us
    pallas_call x4, Pallas kernels, local(): pl.pallas_call(functools.partial(local_kernel, tuple(range(part * count,...  9.85 us
    ppermute x2, waiting for transfers between devices, shards(): lax.ppermute(pay, 'ctx', [(i, i + 2 * step) for i in range(blocks - 2 * s...  9.35 us
    ppermute x5, starting transfers between devices, shards(): summed = summed + lax.ppermute(piece, 'exp', perm).astype(F32)  5.9 us
    unnamed x12, local copies, waits for them, and re-layouts  4.84 us
    pallas_call x2, Pallas kernels, states(): pl.pallas_call(functools.partial(state_kernel, half, width), grid_spec=pl...  4.08 us
    ppermute x5, waiting for transfers between devices, shards(): summed = summed + lax.ppermute(piece, 'exp', perm).astype(F32)  4.04 us
    ppermute x2, starting transfers between devices, shards(): lax.ppermute(pay, 'ctx', [(i, i + 2 * step) for i in range(blocks - 2 * s...  2.57 us
  transfers between devices with their start and end apart: 11, of which 6 were waited for; matrix products, arithmetic and copies ran while one was open for 1% of the time, Pallas kernels for 48%

profile of v2, /device:TPU:24, one launch (start us, length us, event | category | flops | bytes accessed | tf_op | source)
XLA Modules:
  0.0 72.9 jit_solution(12433259421619606539)
XLA Ops:
  0.0 0.0 collective-permute-start.5
  0.0 0.7 copy-done.1
  0.7 2.2 %states.3 = (bf16[528,128]{1,0:T(8,128)(2,1)S(1)}, f32[8,512]{1,0:T(8,128)}) custom-call(s32[1]{0:T(128)} %bitcast.4.which_ref, f32[8,512]{1,0:T(8,128)S(1)} %bitcast.6, bf16[512,1024]{1,0:T(8,128)(2,1)} %k_ref.7, bf16[512,1024]{1,0:T(8,128)(2,1)} %v_ref.7), custom_call_target="tpu_custom_call" | custom-call | tf_op jit(solution)/shard_map/states/pallas_call | solution.py:101
  2.9 1.5 %collective-permute-start = (bf16[528,128]{1,0:T(8,128)(2,1)S(1)}, bf16[528,128]{1,0:T(8,128)(2,1)S(1)}, u32[]{:S(2)}, u32[]{:S(2)}) collective-permute-start(bf16[528,128]{1,0:T(8,128)(2,1)S(1)} %get-tuple-element.34), channel_id=1, source_target_pairs={{0,4},{4,0},{8,12},{12,8},{16,20},{20,16},{24,28},{28,24},{1,5},{5... | collective-permute-start | bytes 405512 | tf_op jit(solution)/shard_map/ppermute | solution.py:395
  4.4 0.7 copy-done.2
  5.1 1.9 %states.2 = (f32[528,128]{1,0:T(8,128)S(1)}, f32[8,512]{1,0:T(8,128)S(1)}) custom-call(s32[1]{0:T(128)} %bitcast.2.which_ref.side_ref, f32[8,512]{1,0:T(8,128)S(1)} %bitcast.7, bf16[512,1024]{1,0:T(8,128)(2,1)} %k_ref.7, bf16[512,1024]{1,0:T(8,128)(2,1)} %v_ref.7), custom_call_target="tpu_custom_call" | custom-call | tf_op jit(solution)/shard_map/states/pallas_call | solution.py:101
  7.0 0.0 copy-start.3
  7.0 1.8 %collective-permute-done.met_ref = bf16[528,128]{1,0:T(8,128)(2,1)S(1)} collective-permute-done((bf16[528,128]{1,0:T(8,128)(2,1)S(1)}, bf16[528,128]{1,0:T(8,128)(2,1)S(1)}, u32[]{:S(2)}, u32[]{:S(2)}) %collective-permute-start) | collective-permute-done | bytes 135200 | tf_op jit(solution)/shard_map/ppermute | solution.py:395
  8.9 0.1 pair.1
  8.9 1.3 %collective-permute-start.1 = (bf16[528,128]{1,0:T(8,128)(2,1)S(1)}, bf16[528,128]{1,0:T(8,128)(2,1)S(1)}, u32[]{:S(2)}, u32[]{:S(2)}) collective-permute-start(bf16[528,128]{1,0:T(8,128)(2,1)S(1)} %get-tuple-element.35.hold_ref), channel_id=1, source_target_pairs={{0,8},{4,12},{8,16},{12,20},{16,24},{20,28},{1,9},{5,13},{9,17},{1... | collective-permute-start | bytes 405512 | tf_op jit(solution)/shard_map/ppermute | solution.py:413
  10.2 2.5 %local.4 = (f32[512,256]{1,0:T(8,128)S(1)}, bf16[512,256]{1,0:T(8,128)(2,1)S(1)}) custom-call(f32[8,512]{1,0:T(8,128)S(1)} %get-tuple-element.37.cum_ref, bf16[512,1024]{1,0:T(8,128)(2,1)} %q_ref.7, bf16[512,1024]{1,0:T(8,128)(2,1)} %k_ref.7, bf16[512,1024]{1,0:T(8,128)(2,1)} %v_ref.7, bf16[528,128]{1,0:T(8,128)(2,1)S(1)} %get-tuple-element.35.hold_ref), custom_call_target="tpu_custom_call" | custom-call | tf_op jit(solution)/shard_map/local/pallas_call | solution.py:293
  12.7 3.3 %collective-permute-done.1.got_ref = bf16[528,128]{1,0:T(8,128)(2,1)S(1)} collective-permute-done((bf16[528,128]{1,0:T(8,128)(2,1)S(1)}, bf16[528,128]{1,0:T(8,128)(2,1)S(1)}, u32[]{:S(2)}, u32[]{:S(2)}) %collective-permute-start.1) | collective-permute-done | bytes 135200 | tf_op jit(solution)/shard_map/ppermute | solution.py:413
  16.0 0.8 %widen.1 = (bf16[528,128]{1,0:T(8,128)(2,1)S(1)}, f32[528,128]{1,0:T(8,128)}, f32[528,128]{1,0:T(8,128)S(1)}) custom-call(bf16[528,128]{1,0:T(8,128)(2,1)S(1)} %collective-permute-done.1.got_ref, f32[528,128]{1,0:T(8,128)S(1)} %get-tuple-element.36.window_ref.before_ref, f32[528,128]{1,0:T(8,128)S(1)} %get-tuple-element.36.window_ref.before_ref, ...), custom_call_target="tpu_custom_call" | custom-call | tf_op jit(solution)/shard_map/widen/pallas_call | solution.py:203
  16.7 1.3 %collective-permute-start.2 = (bf16[528,128]{1,0:T(8,128)(2,1)S(1)}, bf16[528,128]{1,0:T(8,128)(2,1)S(1)}, u32[]{:S(2)}, u32[]{:S(2)}) collective-permute-start(bf16[528,128]{1,0:T(8,128)(2,1)S(1)} %get-tuple-element.39.hold_ref), channel_id=1, source_target_pairs={{0,16},{4,20},{8,24},{12,28},{1,17},{5,21},{9,25},{13,29},{2,18},{... | collective-permute-start | bytes 405512 | tf_op jit(solution)/shard_map/ppermute | solution.py:413
  18.0 2.5 %local.5 = (f32[512,256]{1,0:T(8,128)S(1)}, bf16[512,256]{1,0:T(8,128)(2,1)S(1)}) custom-call(f32[8,512]{1,0:T(8,128)S(1)} %get-tuple-element.37.cum_ref, bf16[512,1024]{1,0:T(8,128)(2,1)} %q_ref.7, bf16[512,1024]{1,0:T(8,128)(2,1)} %k_ref.7, bf16[512,1024]{1,0:T(8,128)(2,1)} %v_ref.7, bf16[528,128]{1,0:T(8,128)(2,1)S(1)} %get-tuple-element.39.hold_ref), custom_call_target="tpu_custom_call" | custom-call | tf_op jit(solution)/shard_map/local/pallas_call | solution.py:293
  20.5 6.1 %collective-permute-done.2.got_ref = bf16[528,128]{1,0:T(8,128)(2,1)S(1)} collective-permute-done((bf16[528,128]{1,0:T(8,128)(2,1)S(1)}, bf16[528,128]{1,0:T(8,128)(2,1)S(1)}, u32[]{:S(2)}, u32[]{:S(2)}) %collective-permute-start.2) | collective-permute-done | bytes 135200 | tf_op jit(solution)/shard_map/ppermute | solution.py:413
  26.6 0.1 enter.1
  26.7 1.6 %collective-permute-start.3 = (bf16[512,128]{1,0:T(8,128)(2,1)S(1)}, bf16[512,128]{1,0:T(8,128)(2,1)S(1)}, u32[]{:S(2)}, u32[]{:S(2)}) collective-permute-start(bf16[512,128]{1,0:T(8,128)(2,1)S(1)} %get-tuple-element.44.hold_ref), channel_id=1, source_target_pairs={{0,4},{4,0},{8,12},{12,8},{16,20},{20,16},{24,28},{28,24},{1,5},{5... | collective-permute-start | bytes 393224 | tf_op jit(solution)/shard_map/ppermute | solution.py:420
  28.2 0.1 pad_add_fusion.spot_ref
  28.3 2.5 %local.6 = (f32[512,256]{1,0:T(8,128)S(1)}, bf16[512,256]{1,0:T(8,128)(2,1)S(1)}) custom-call(f32[8,512]{1,0:T(8,128)S(1)} %get-tuple-element.37.cum_ref, bf16[512,1024]{1,0:T(8,128)(2,1)} %q_ref.7, bf16[512,1024]{1,0:T(8,128)(2,1)} %k_ref.7, bf16[512,1024]{1,0:T(8,128)(2,1)} %v_ref.7, bf16[512,128]{1,0:T(8,128)(2,1)S(1)} %get-tuple-element.44.hold_ref), custom_call_target="tpu_custom_call" | custom-call | tf_op jit(solution)/shard_map/local/pallas_call | solution.py:293
  30.8 2.5 %local.7 = (f32[512,256]{1,0:T(8,128)S(1)}, bf16[512,256]{1,0:T(8,128)(2,1)S(1)}) custom-call(f32[8,512]{1,0:T(8,128)S(1)} %get-tuple-element.37.cum_ref, bf16[512,1024]{1,0:T(8,128)(2,1)} %q_ref.7, bf16[512,1024]{1,0:T(8,128)(2,1)} %k_ref.7, bf16[512,1024]{1,0:T(8,128)(2,1)} %v_ref.7, bf16[512,128]{1,0:T(8,128)(2,1)S(1)} %get-tuple-element.44.hold_ref), custom_call_target="tpu_custom_call" | custom-call | tf_op jit(solution)/shard_map/local/pallas_call | solution.py:293
  33.2 0.0 collective-permute-done.3.met_ref
  33.3 1.1 %norm_away.1 = bf16[256,1024]{1,0:T(8,128)(2,1)S(1)} custom-call(s32[3]{0:T(128)S(1)} %pad_add_fusion.spot_ref, bf16[512,128]{1,0:T(8,128)(2,1)S(1)} %get-tuple-element.43.mine_ref, bf16[512,128]{1,0:T(8,128)(2,1)S(1)} %collective-permute-done.3.met_ref, f32[1,1024]{1,0:T(1,128)S(1)} %bitcast.8, f32[512,256]{1,0:T(8,128)S(1)} %get-tuple-element.38.hold_ref.refs_0_, ...), custom_call_target="tpu_custom_call" | custom-call | tf_op jit(solution)/shard_map/norm_away/pallas_call | solution.py:337
  34.4 0.1 collective-permute-start.4
  34.4 1.1 %norm_home.1.mine_ref = bf16[256,1024]{1,0:T(8,128)(2,1)S(1)} custom-call(s32[3]{0:T(128)S(1)} %pad_add_fusion.spot_ref, bf16[512,128]{1,0:T(8,128)(2,1)S(1)} %get-tuple-element.43.mine_ref, bf16[512,128]{1,0:T(8,128)(2,1)S(1)} %collective-permute-done.3.met_ref, f32[1,1024]{1,0:T(1,128)S(1)} %bitcast.9, f32[512,256]{1,0:T(8,128)S(1)} %get-tuple-element.38.hold_ref.refs_0_, ...), custom_call_target="tpu_custom_call" | custom-call | tf_op jit(solution)/shard_map/norm_home/pallas_call | solution.py:337
  35.5 0.8 %collective-permute-done.4.other_ref = bf16[256,1024]{1,0:T(8,128)(2,1)S(1)} collective-permute-done((bf16[256,1024]{1,0:T(8,128)(2,1)S(1)}, bf16[256,1024]{1,0:T(8,128)(2,1)S(1)}, u32[]{:S(2)}, u32[]{:S(2)}) %collective-permute-start.4) | collective-permute-done | bytes 524320 | tf_op jit(solution)/shard_map/ppermute | solution.py:429
  36.3 0.0 collective-permute-done.5.far_ref
  36.3 3.4 %copy-done = bf16[1024,4096]{1,0:T(8,128)(2,1)S(1)} copy-done((bf16[1024,4096]{1,0:T(8,128)(2,1)S(1)}, bf16[1024,4096]{1,0:T(8,128)(2,1)}, u32[]{:S(2)}) %copy-start) | copy-done | bytes 8388632
  39.7 4.1 %project.5 = (f32[128,512]{1,0:T(8,128)S(1)}, bf16[128,512]{1,0:T(8,128)(2,1)S(1)}) custom-call(bf16[256,1024]{1,0:T(8,128)(2,1)S(1)} %norm_home.1.mine_ref, bf16[256,1024]{1,0:T(8,128)(2,1)S(1)} %collective-permute-done.4.other_ref, bf16[1024,4096]{1,0:T(8,128)(2,1)S(1)} %copy-done, bf16[1024,4096]{1,0:T(8,128)(2,1)} %collective-permute-done.5.far_ref), custom_call_target="tpu_custom_call" | custom-call | tf_op jit(solution)/shard_map/project/pallas_call | solution.py:360
  43.8 1.6 %collective-permute-start.6 = (bf16[128,512]{1,0:T(8,128)(2,1)S(1)}, bf16[128,512]{1,0:T(8,128)(2,1)S(1)}, u32[]{:S(2)}, u32[]{:S(2)}) collective-permute-start(bf16[128,512]{1,0:T(8,128)(2,1)S(1)} %get-tuple-element.52), channel_id=1, source_target_pairs={{0,2},{1,3},{2,0},{3,1},{4,6},{5,7},{6,4},{7,5},{8,10},{9,11},{10,... | collective-permute-start | bytes 393224 | tf_op jit(solution)/shard_map/ppermute | solution.py:445
  45.4 4.6 %project.6 = (f32[128,1024]{1,0:T(8,128)S(1)}, bf16[128,1024]{1,0:T(8,128)(2,1)S(1)}) custom-call(bf16[256,1024]{1,0:T(8,128)(2,1)S(1)} %norm_home.1.mine_ref, bf16[256,1024]{1,0:T(8,128)(2,1)S(1)} %collective-permute-done.4.other_ref, bf16[1024,4096]{1,0:T(8,128)(2,1)S(1)} %copy-done, bf16[1024,4096]{1,0:T(8,128)(2,1)} %collective-permute-done.5.far_ref), custom_call_target="tpu_custom_call" | custom-call | tf_op jit(solution)/shard_map/project/pallas_call | solution.py:360
  50.0 0.6 collective-permute-start.7
  50.6 4.6 %project.7 = (f32[128,1024]{1,0:T(8,128)S(1)}, bf16[128,1024]{1,0:T(8,128)(2,1)S(1)}) custom-call(bf16[256,1024]{1,0:T(8,128)(2,1)S(1)} %norm_home.1.mine_ref, bf16[256,1024]{1,0:T(8,128)(2,1)S(1)} %collective-permute-done.4.other_ref, bf16[1024,4096]{1,0:T(8,128)(2,1)S(1)} %copy-done, bf16[1024,4096]{1,0:T(8,128)(2,1)} %collective-permute-done.5.far_ref), custom_call_target="tpu_custom_call" | custom-call | tf_op jit(solution)/shard_map/project/pallas_call | solution.py:360
  55.2 1.6 %collective-permute-start.8 = (bf16[128,1024]{1,0:T(8,128)(2,1)S(1)}, bf16[128,1024]{1,0:T(8,128)(2,1)S(1)}, u32[]{:S(2)}, u32[]{:S(2)}) collective-permute-start(bf16[128,1024]{1,0:T(8,128)(2,1)S(1)} %get-tuple-element.56), channel_id=1, source_target_pairs={{0,2},{1,3},{2,0},{3,1},{4,6},{5,7},{6,4},{7,5},{8,10},{9,11},{10,... | collective-permute-start | bytes 786440 | tf_op jit(solution)/shard_map/ppermute | solution.py:445
  56.8 4.6 %project.8 = (f32[128,1024]{1,0:T(8,128)S(1)}, bf16[128,1024]{1,0:T(8,128)(2,1)S(1)}) custom-call(bf16[256,1024]{1,0:T(8,128)(2,1)S(1)} %norm_home.1.mine_ref, bf16[256,1024]{1,0:T(8,128)(2,1)S(1)} %collective-permute-done.4.other_ref, bf16[1024,4096]{1,0:T(8,128)(2,1)S(1)} %copy-done, bf16[1024,4096]{1,0:T(8,128)(2,1)} %collective-permute-done.5.far_ref), custom_call_target="tpu_custom_call" | custom-call | tf_op jit(solution)/shard_map/project/pallas_call | solution.py:360
  61.4 0.0 copy-start.4
  61.4 0.6 collective-permute-start.9
  62.0 4.1 %project.9 = (f32[128,512]{1,0:T(8,128)S(1)}, bf16[128,512]{1,0:T(8,128)(2,1)S(1)}) custom-call(bf16[256,1024]{1,0:T(8,128)(2,1)S(1)} %norm_home.1.mine_ref, bf16[256,1024]{1,0:T(8,128)(2,1)S(1)} %collective-permute-done.4.other_ref, bf16[1024,4096]{1,0:T(8,128)(2,1)S(1)} %copy-done, bf16[1024,4096]{1,0:T(8,128)(2,1)} %collective-permute-done.5.far_ref), custom_call_target="tpu_custom_call" | custom-call | tf_op jit(solution)/shard_map/project/pallas_call | solution.py:360
  66.1 1.6 %collective-permute-start.10 = (bf16[128,512]{1,0:T(8,128)(2,1)S(1)}, bf16[128,512]{1,0:T(8,128)(2,1)S(1)}, u32[]{:S(2)}, u32[]{:S(2)}) collective-permute-start(bf16[128,512]{1,0:T(8,128)(2,1)S(1)} %get-tuple-element.60), channel_id=1, source_target_pairs={{0,2},{1,3},{2,0},{3,1},{4,6},{5,7},{6,4},{7,5},{8,10},{9,11},{10,... | collective-permute-start | bytes 393224 | tf_op jit(solution)/shard_map/ppermute | solution.py:445
  67.8 0.1 dynamic_update_slice.15
  67.9 0.0 collective-permute-done.7
  67.9 0.1 fusion
  68.0 0.1 fusion.1
  68.1 2.6 %collective-permute-done.9 = bf16[128,1024]{1,0:T(8,128)(2,1)S(1)} collective-permute-done((bf16[128,1024]{1,0:T(8,128)(2,1)S(1)}, bf16[128,1024]{1,0:T(8,128)(2,1)S(1)}, u32[]{:S(2)}, u32[]{:S(2)}) %collective-permute-start.9) | collective-permute-done | bytes 262176 | tf_op jit(solution)/shard_map/ppermute | solution.py:445
  70.7 0.1 fusion.2
  70.8 0.0 copy-start.5
  70.8 1.4 %collective-permute-done.10 = bf16[128,512]{1,0:T(8,128)(2,1)S(1)} collective-permute-done((bf16[128,512]{1,0:T(8,128)(2,1)S(1)}, bf16[128,512]{1,0:T(8,128)(2,1)S(1)}, u32[]{:S(2)}, u32[]{:S(2)}) %collective-permute-start.10) | collective-permute-done | bytes 131104 | tf_op jit(solution)/shard_map/ppermute | solution.py:445
  72.2 0.7 fusion.3
  (9 shorter events, 0.1 us)
Async XLA Ops:
  0.0 36.3 %collective-permute-start.5 = (bf16[1024,4096]{1,0:T(8,128)(2,1)}, bf16[1024,4096]{1,0:T(8,128)(2,1)}, u32[]{:S(2)}, u32[]{:S(2)}) collective-permute-start(bf16[1024,4096]{1,0:T(8,128)(2,1)} %near_ref.9), channel_id=1, source_target_pairs={{0,1},{1,0},{2,3},{3,2},{4,5},{5,4},{6,7},{7,6},{8,9},{9,8},{10,11... | collective-permute-start | bytes 25165832 | tf_op jit(solution)/shard_map/ppermute | solution.py:396
  0.0 0.7 copy-start.1
  2.9 6.0 %collective-permute-start = (bf16[528,128]{1,0:T(8,128)(2,1)S(1)}, bf16[528,128]{1,0:T(8,128)(2,1)S(1)}, u32[]{:S(2)}, u32[]{:S(2)}) collective-permute-start(bf16[528,128]{1,0:T(8,128)(2,1)S(1)} %get-tuple-element.34), channel_id=1, source_target_pairs={{0,4},{4,0},{8,12},{12,8},{16,20},{20,16},{24,28},{28,24},{1,5},{5... | collective-permute-start | bytes 405512 | tf_op jit(solution)/shard_map/ppermute | solution.py:395
  4.4 0.7 copy-start.2
  7.0 26.2 %copy-start.3 = (f32[1024]{0:T(1024)S(1)}, f32[1024]{0:T(1024)}, u32[]{:S(2)}) copy-start(f32[1024]{0:T(1024)} %param.11) | copy-start | bytes 12292
  8.9 7.0 %collective-permute-start.1 = (bf16[528,128]{1,0:T(8,128)(2,1)S(1)}, bf16[528,128]{1,0:T(8,128)(2,1)S(1)}, u32[]{:S(2)}, u32[]{:S(2)}) collective-permute-start(bf16[528,128]{1,0:T(8,128)(2,1)S(1)} %get-tuple-element.35.hold_ref), channel_id=1, source_target_pairs={{0,8},{4,12},{8,16},{12,20},{16,24},{20,28},{1,9},{5,13},{9,17},{1... | collective-permute-start | bytes 405512 | tf_op jit(solution)/shard_map/ppermute | solution.py:413
  16.7 9.8 %collective-permute-start.2 = (bf16[528,128]{1,0:T(8,128)(2,1)S(1)}, bf16[528,128]{1,0:T(8,128)(2,1)S(1)}, u32[]{:S(2)}, u32[]{:S(2)}) collective-permute-start(bf16[528,128]{1,0:T(8,128)(2,1)S(1)} %get-tuple-element.39.hold_ref), channel_id=1, source_target_pairs={{0,16},{4,20},{8,24},{12,28},{1,17},{5,21},{9,25},{13,29},{2,18},{... | collective-permute-start | bytes 405512 | tf_op jit(solution)/shard_map/ppermute | solution.py:413
  26.7 6.6 %collective-permute-start.3 = (bf16[512,128]{1,0:T(8,128)(2,1)S(1)}, bf16[512,128]{1,0:T(8,128)(2,1)S(1)}, u32[]{:S(2)}, u32[]{:S(2)}) collective-permute-start(bf16[512,128]{1,0:T(8,128)(2,1)S(1)} %get-tuple-element.44.hold_ref), channel_id=1, source_target_pairs={{0,4},{4,0},{8,12},{12,8},{16,20},{20,16},{24,28},{28,24},{1,5},{5... | collective-permute-start | bytes 393224 | tf_op jit(solution)/shard_map/ppermute | solution.py:420
  34.4 2.0 %collective-permute-start.4 = (bf16[256,1024]{1,0:T(8,128)(2,1)S(1)}, bf16[256,1024]{1,0:T(8,128)(2,1)S(1)}, u32[]{:S(2)}, u32[]{:S(2)}) collective-permute-start(bf16[256,1024]{1,0:T(8,128)(2,1)S(1)} %norm_away.1), channel_id=1, source_target_pairs={{0,1},{1,0},{2,3},{3,2},{4,5},{5,4},{6,7},{7,6},{8,9},{9,8},{10,11... | collective-permute-start | bytes 1572872 | tf_op jit(solution)/shard_map/ppermute | solution.py:429
  36.3 3.4 %copy-start = (bf16[1024,4096]{1,0:T(8,128)(2,1)S(1)}, bf16[1024,4096]{1,0:T(8,128)(2,1)}, u32[]{:S(2)}) copy-start(bf16[1024,4096]{1,0:T(8,128)(2,1)} %near_ref.9) | copy-start | bytes 25165828
  43.8 23.9 %collective-permute-start.6 = (bf16[128,512]{1,0:T(8,128)(2,1)S(1)}, bf16[128,512]{1,0:T(8,128)(2,1)S(1)}, u32[]{:S(2)}, u32[]{:S(2)}) collective-permute-start(bf16[128,512]{1,0:T(8,128)(2,1)S(1)} %get-tuple-element.52), channel_id=1, source_target_pairs={{0,2},{1,3},{2,0},{3,1},{4,6},{5,7},{6,4},{7,5},{8,10},{9,11},{10,... | collective-permute-start | bytes 393224 | tf_op jit(solution)/shard_map/ppermute | solution.py:445
  50.0 17.8 %collective-permute-start.7 = (bf16[128,1024]{1,0:T(8,128)(2,1)S(1)}, bf16[128,1024]{1,0:T(8,128)(2,1)S(1)}, u32[]{:S(2)}, u32[]{:S(2)}) collective-permute-start(bf16[128,1024]{1,0:T(8,128)(2,1)S(1)} %get-tuple-element.54), channel_id=1, source_target_pairs={{0,2},{1,3},{2,0},{3,1},{4,6},{5,7},{6,4},{7,5},{8,10},{9,11},{10,... | collective-permute-start | bytes 786440 | tf_op jit(solution)/shard_map/ppermute | solution.py:445
  55.2 12.7 %collective-permute-start.8 = (bf16[128,1024]{1,0:T(8,128)(2,1)S(1)}, bf16[128,1024]{1,0:T(8,128)(2,1)S(1)}, u32[]{:S(2)}, u32[]{:S(2)}) collective-permute-start(bf16[128,1024]{1,0:T(8,128)(2,1)S(1)} %get-tuple-element.56), channel_id=1, source_target_pairs={{0,2},{1,3},{2,0},{3,1},{4,6},{5,7},{6,4},{7,5},{8,10},{9,11},{10,... | collective-permute-start | bytes 786440 | tf_op jit(solution)/shard_map/ppermute | solution.py:445
  61.4 6.3 %copy-start.4 = (bf16[128,4096]{1,0:T(8,128)(2,1)S(1)}, bf16[128,4096]{1,0:T(8,128)(2,1)}, u32[]{:S(2)}) copy-start(bf16[128,4096]{1,0:T(8,128)(2,1)} %param.13) | copy-start | bytes 3145732
  61.4 9.2 %collective-permute-start.9 = (bf16[128,1024]{1,0:T(8,128)(2,1)S(1)}, bf16[128,1024]{1,0:T(8,128)(2,1)S(1)}, u32[]{:S(2)}, u32[]{:S(2)}) collective-permute-start(bf16[128,1024]{1,0:T(8,128)(2,1)S(1)} %get-tuple-element.58), channel_id=1, source_target_pairs={{0,2},{1,3},{2,0},{3,1},{4,6},{5,7},{6,4},{7,5},{8,10},{9,11},{10,... | collective-permute-start | bytes 786440 | tf_op jit(solution)/shard_map/ppermute | solution.py:445
  66.1 6.1 %collective-permute-start.10 = (bf16[128,512]{1,0:T(8,128)(2,1)S(1)}, bf16[128,512]{1,0:T(8,128)(2,1)S(1)}, u32[]{:S(2)}, u32[]{:S(2)}) collective-permute-start(bf16[128,512]{1,0:T(8,128)(2,1)S(1)} %get-tuple-element.60), channel_id=1, source_target_pairs={{0,2},{1,3},{2,0},{3,1},{4,6},{5,7},{6,4},{7,5},{8,10},{9,11},{10,... | collective-permute-start | bytes 393224 | tf_op jit(solution)/shard_map/ppermute | solution.py:445
  70.8 1.4 %copy-start.5 = (bf16[128,4096]{1,0:T(8,128)(2,1)}, bf16[128,4096]{1,0:T(8,128)(2,1)S(1)}, u32[]{:S(2)}) copy-start(bf16[128,4096]{1,0:T(8,128)(2,1)S(1)} %fusion.2) | copy-start | bytes 3145732

commit v3 on v2

--- a/solution.py
+++ b/solution.py
@@ -63,7 +63,7 @@
     return jnp.concatenate(done, axis=1)
 
 
-def state_kernel(half, width, which_ref, logd_ref, key_ref, value_ref, pay_ref, cum_ref):
+def state_kernel(half, width, which_ref, logd_ref, key_ref, value_ref, hold_ref, pay_ref, cum_ref):
     second = which_ref[0] == 1
     cum = running_sum(logd_ref[...])
     cum_ref[...] = cum
@@ -94,7 +94,7 @@
     pay_ref[base:, :] = tail.astype(pay_ref.dtype)
 
 
-def states(which, logd, key, value, half, width, kind):
+def states(which, logd, key, value, hold, half, width, kind):
     heads, rows = logd.shape
     cols = half * width
     tall = cols + 2 * pad_rows(half)
@@ -107,6 +107,7 @@
                 pl.BlockSpec((heads, rows), lambda i, w: (0, 0)),
                 pl.BlockSpec((rows, cols), lambda i, w: (0, w[0])),
                 pl.BlockSpec((rows, cols), lambda i, w: (0, w[0])),
+                ANY,
             ],
             out_specs=[VMEM, VMEM],
         ),
@@ -116,7 +117,7 @@
         ],
         compiler_params=PARAMS,
         name="states",
-    )(which, logd, outside(key), outside(value))
+    )(which, outside(logd), outside(key), outside(value), hold)
 
 
 def decay_row(pay, j, half, width):
@@ -174,12 +175,15 @@
     )(side, near(own), near(met))
 
 
-def widen_kernel(half, width, opening, got_ref, window_ref, before_ref, hold_ref, pay_ref, wide_ref, past_ref):
+def widen_kernel(half, width, opening, got_ref, early_ref, window_ref, before_ref, hold_ref, pay_ref, wide_ref, past_ref):
     decays, pasts = [], []
     for j in range(half):
         rows = slice(j * width, (j + 1) * width)
         got = got_ref[rows, :].astype(F32)
         got_decay = decay_row(got_ref, j, half, width)
+        if not opening:
+            got = got + early_ref[rows, :].astype(F32)
+            got_decay = got_decay + decay_row(early_ref, j, half, width)
         window_decay = decay_row(window_ref, j, half, width)
         wide = got * window_decay + window_ref[rows, :]
         wide_ref[rows, :] = wide
@@ -197,12 +201,14 @@
     put_decays(past_ref, pasts, half, width)
 
 
-def widen(got, window, before, hold, half, width):
+def widen(got, early, window, before, hold, half, width):
     shape = window.shape
     opening = before is None
+    early = got if opening else early
+    before = window if opening else before
     return pl.pallas_call(
         functools.partial(widen_kernel, half, width, opening),
-        in_specs=[VMEM, VMEM, VMEM, ANY],
+        in_specs=[VMEM, VMEM, VMEM, VMEM, ANY],
         out_specs=[VMEM, VMEM, VMEM],
         out_shape=[
             held(shape, BF16),
@@ -211,10 +217,10 @@
         ],
         compiler_params=PARAMS,
         name="widen",
-    )(near(got), near(window), near(window if opening else before), hold)
-
-
-def enter_kernel(half, width, rounds, side_ref, got_ref, before_ref, first_ref, hold_ref, mine_ref, theirs_ref):
+    )(near(got), near(early), near(window), near(before), hold)
+
+
+def enter_kernel(half, width, rounds, side_ref, got_ref, early_ref, before_ref, first_ref, hold_ref, mine_ref, theirs_ref):
     is_first = side_ref[0] == 0
     for j in range(half):
         rows = slice(j * width, (j + 1) * width)
@@ -223,27 +229,38 @@
         else:
             before = got_ref[rows, :].astype(F32)
             if rounds > 1:
+                before = before + early_ref[rows, :].astype(F32)
                 before = before * decay_row(before_ref, j, half, width) + before_ref[rows, :]
         after = before * decay_row(first_ref, j, half, width) + first_ref[rows, :]
         mine_ref[rows, :] = jnp.where(is_first, before, after).astype(BF16)
         theirs_ref[rows, :] = jnp.where(is_first, after, before).astype(BF16)
 
 
-def enter(side, got, before, first, hold, half, width, rounds):
+def enter(side, got, early, before, first, hold, half, width, rounds):
     shape = (half * width, width)
     got = first if got is None else got
+    early = first if early is None else early
     before = first if before is None else before
     return pl.pallas_call(
         functools.partial(enter_kernel, half, width, rounds),
-        in_specs=[SMEM, VMEM, VMEM, VMEM, ANY],
+        in_specs=[SMEM, VMEM, VMEM, VMEM, VMEM, ANY],
         out_specs=[VMEM, VMEM],
         out_shape=[held(shape, BF16)] * 2,
         compiler_params=PARAMS,
         name="enter",
-    )(side, near(got), near(before), near(first), hold)
-
-
-def local_kernel(heads, width, cum_ref, q_ref, k_ref, v_ref, hold_ref, out_ref, decayed_ref):
+    )(side, near(got), near(early), near(before), near(first), hold)
+
+
+def local_kernel(heads, width, cum_ref, q_ref, k_ref, v_ref, hold_ref, *refs):
+    copies = []
+    count = len(refs) // 3 if len(refs) > 2 else 0
+    out_ref, decayed_ref = refs[count : count + 2]
+    for i in range(count):
+        target = refs[count + 2 + i]
+        source = refs[i].at[:, pl.ds(0, target.shape[1])]
+        copies.append(pltpu.make_async_copy(source, target, refs[2 * count + 2 + i]))
+    for copy in copies:
+        copy.start()
     rows = cum_ref.shape[1]
     tile = tile_of(rows, width)
     causal = lax.broadcasted_iota(jnp.int32, (tile, tile), 0) >= lax.broadcasted_iota(
@@ -274,18 +291,21 @@
                     query, k_ref[earlier, cols], (((1,), (1,)), ((), ())), preferred_element_type=F32
                 )
                 weight = jnp.exp(edge - cum[:, earlier])
-                out = out + since[:, :1] * jnp.dot(
-                    (scores * weight).astype(BF16), v_ref[earlier, cols], preferred_element_type=F32
-                ) if tile != width else out + since * jnp.dot(
+                if tile != width:
+                    since = since[:, :1]
+                out = out + since * jnp.dot(
                     (scores * weight).astype(BF16), v_ref[earlier, cols], preferred_element_type=F32
                 )
                 decay = since * jnp.exp(edge)
             out_ref[here, cols] = out
-            decay = decay if tile == width else decay[:, :1]
+            if tile != width:
+                decay = decay[:, :1]
             decayed_ref[here, cols] = (query.astype(F32) * decay).astype(BF16)
-
-
-def local(cum, query, key, value, hold, part, parts, heads, width):
+    for copy in copies:
+        copy.wait()
+
+
+def local(cum, query, key, value, hold, extra, columns, part, parts, heads, width):
     rows = cum.shape[1]
     count = heads // parts
     cols = count * width
@@ -293,15 +313,17 @@
     return pl.pallas_call(
         functools.partial(local_kernel, tuple(range(part * count, (part + 1) * count)), width),
         grid=(1,),
-        in_specs=[VMEM, block, block, block, ANY],
-        out_specs=[VMEM, VMEM],
+        in_specs=[VMEM, block, block, block, ANY] + [ANY] * len(extra),
+        out_specs=[VMEM, VMEM] + [VMEM] * len(extra),
         out_shape=[
             held((rows, cols), F32),
             held((rows, cols), BF16),
-        ],
+        ]
+        + [held((a.shape[0], columns), a.dtype) for a in extra],
+        scratch_shapes=[pltpu.SemaphoreType.DMA] * len(extra),
         compiler_params=PARAMS,
         name="local",
-    )(near(cum), outside(query), outside(key), outside(value), hold)
+    )(near(cum), outside(query), outside(key), outside(value), hold, *map(outside, extra))
 
 
 def norm_kernel(half, width, parts, chips, block, away, spot_ref, mine_ref, met_ref, gain_ref, *refs):
@@ -344,35 +366,41 @@
     )(spot, near(mine), near(met), gain, *map(near, insides), *map(near, queries))
 
 
-def project_kernel(block, first, tile, mine_ref, other_ref, near_ref, far_ref, own_ref, away_ref):
-    for i in range(own_ref.shape[1] // tile):
-        cols = slice(first + i * tile, first + (i + 1) * tile)
-        total = jnp.dot(mine_ref[...], near_ref[:, cols], preferred_element_type=F32) + jnp.dot(
-            other_ref[...], far_ref[:, cols], preferred_element_type=F32
-        )
-        span = slice(i * tile, (i + 1) * tile)
-        own_ref[:, span] = total[:block]
-        away_ref[:, span] = total[block:].astype(away_ref.dtype)
-
-
-def project(mine, other, first_weight, second_weight, block, first, count, tile):
+def project_kernel(block, mine_ref, other_ref, near_ref, far_ref, hold_ref, own_ref, away_ref):
+    total = jnp.dot(mine_ref[...], near_ref[...], preferred_element_type=F32) + jnp.dot(
+        other_ref[...], far_ref[...], preferred_element_type=F32
+    )
+    own_ref[...] = total[:block]
+    away_ref[...] = total[block:].astype(away_ref.dtype)
+
+
+def project(mine, other, first_weight, second_weight, hold, block, first, count, tile):
     rows, depth = mine.shape
-    return pl.pallas_call(
-        functools.partial(project_kernel, block, first, tile),
-        in_specs=[
-            VMEM,
-            VMEM,
-            VMEM,
-            VMEM,
+    start = first // tile
+    at_hand = hold is None
+    span = pl.BlockSpec((depth, tile), lambda i: (0, start + i))
+    place = near if at_hand else outside
+    return pl.pallas_call(
+        functools.partial(project_kernel, block),
+        grid=(count // tile,),
+        in_specs=[VMEM, VMEM] + [VMEM if at_hand else span] * 2 + [ANY],
+        out_specs=[
+            pl.BlockSpec((block, tile), lambda i: (0, i)),
+            pl.BlockSpec((rows - block, tile), lambda i: (0, i)),
         ],
-        out_specs=[VMEM, VMEM],
         out_shape=[
             held((block, count), F32),
             held((rows - block, count), BF16),
         ],
         compiler_params=PARAMS,
         name="project",
-    )(near(mine), near(other), near(first_weight), near(second_weight))
+    )(
+        near(mine),
+        near(other),
+        place(first_weight),
+        place(second_weight),
+        mine if at_hand else hold,
+    )
 
 
 def shards(blocks, group, q_spikes, k_spikes, v_spikes, log_decay, norm_gain, out_weight, residual):
@@ -391,35 +419,50 @@
     logd = log_decay.T
     if heads % 8:
         logd = jnp.pad(logd, ((0, pad_rows(heads) - heads), (0, 0)))
-    sent, _ = states((1 - side).reshape(1), logd, k_spikes, v_spikes, half, width, BF16)
+    sent, _ = states((1 - side).reshape(1), logd, k_spikes, v_spikes, v_spikes, half, width, BF16)
     met = lax.ppermute(sent, "ctx", swap)
-    far_weight = lax.ppermute(out_weight, "exp", cores)
     side = side.reshape(1)
-    kept, cum = states(side, logd, k_spikes, v_spikes, half, width, F32)
-
-    inner = []
-
-    def more(hold):
-        if len(inner) < parts:
-            inner.append(
-                local(cum, q_spikes, k_spikes, v_spikes, hold, len(inner), parts, heads, width)
+    kept, cum = states(side, logd, k_spikes, v_spikes, sent, half, width, F32)
+    kept, weight = lax.optimization_barrier((kept, out_weight))
+    far_weight = lax.ppermute(weight, "exp", cores)
+    total = out_weight.shape[1]
+    tile = tile_of(total, 512)
+
+    inner, weights = [], []
+
+    def more(hold, count):
+        for _ in range(min(count, parts - len(inner))):
+            part = len(inner)
+            extra = [out_weight, far_weight] if part == parts - 1 else []
+            done = local(
+                cum, q_spikes, k_spikes, v_spikes, hold, extra, tile, part, parts, heads, width
             )
-        return inner[-1][0]
+            inner.append(done[:2])
+            weights.extend(done[2:])
+            hold = done[0]
+        return hold
 
     pay, window, first = pair(side, kept, met, half, width)
-    before, got, rounds, step = None, None, 0, 1
+    before, got, early, rounds, step = None, None, None, 0, 1
     hold = pay
     while 2 * step < blocks:
-        got = lax.ppermute(pay, "ctx", [(i, i + 2 * step) for i in range(blocks - 2 * step)])
-        hold = more(pay)
+        pairs = [(i, i + 2 * step) for i in range(step // 2 * 2, blocks - 2 * step)]
+        got = lax.ppermute(pay, "ctx", pairs)
+        last = 4 * step >= blocks
+        ahead = None
+        if not last:
+            ahead = lax.ppermute(
+                pay, "ctx", [(i, i + 4 * step) for i in range(min(2 * step, blocks - 4 * step))]
+            )
+        hold = more(pay, parts - len(inner) - 1 if last else 1)
         rounds += 1
         step *= 2
-        if 2 * step < blocks:
-            pay, window, before = widen(got, window, before, hold, half, width)
-    mine, theirs = enter(side, got, before, first, hold, half, width, rounds)
+        if not last:
+            pay, window, before = widen(got, early, window, before, hold, half, width)
+            early = ahead
+    mine, theirs = enter(side, got, early, before, first, hold, half, width, rounds)
     met = lax.ppermute(theirs, "ctx", swap)
-    while len(inner) < parts:
-        more(theirs)
+    more(theirs, parts)
 
     spot = jnp.stack([member >> 1, member & 1, place & 1]).astype(jnp.int32)
     gain = norm_gain.reshape(1, heads * width)
@@ -429,15 +472,14 @@
     other = lax.ppermute(away, "exp", cores)
     home = norm(*args, False)
 
-    total = out_weight.shape[1]
-    tile = tile_of(total, 512)
     sizes = [tile]
     while sum(sizes) < total:
         sizes.append(min(2 * tile, max(tile, total - sum(sizes) - tile)))
     out = jnp.zeros((block, total), BF16)
-    at = 0
+    at, hold = 0, None
     for size in sizes:
-        own, pieces = project(home, other, out_weight, far_weight, block, at, size, tile)
+        own, pieces = project(home, other, *weights, hold, block, at, size, tile)
+        weights, hold = (out_weight, far_weight), pieces
         summed = own + residual[:, at : at + size].astype(F32)
         for d in range(1, chips):
             piece = pieces[(d - 1) * block : d * block]

time: 73.5 us -> 65.7 us (0.89)
  the two profiles are of different devices: /device:TPU:24 before, /device:TPU:0 now
where the time goes in v3:
time: 65.7 us; the launch traced here: 65.3 us
  Pallas kernels  30.3 us (46%)
  starting transfers between devices  19.5 us (30%)
  waiting for transfers between devices  14 us (21%)
  other arithmetic  1.07 us (2%)
    pallas_call x5, Pallas kernels, project(): pl.pallas_call(functools.partial(project_kernel, block), grid=(count // t...  12.1 us
    pallas_call x4, Pallas kernels, local(): pl.pallas_call(functools.partial(local_kernel, tuple(range(part * count,...  11.1 us
    ppermute x5, waiting for transfers between devices, shards(): summed = summed + lax.ppermute(piece, 'exp', perm).astype(F32)  9.05 us
    ppermute x5, starting transfers between devices, shards(): summed = summed + lax.ppermute(piece, 'exp', perm).astype(F32)  5.89 us
    ppermute x1, starting transfers between devices, shards(): lax.ppermute(pay, 'ctx', [(i, i + 4 * step) for i in range(min(2 * step,...  4.49 us
    ppermute x2, starting transfers between devices, shards(): got = lax.ppermute(pay, 'ctx', pairs)  4.41 us
    ppermute x1, waiting for transfers between devices, shards(): met = lax.ppermute(sent, 'ctx', swap)  4.17 us
    pallas_call x2, Pallas kernels, states(): pl.pallas_call(functools.partial(state_kernel, half, width), grid_spec=pl...  4.11 us
  transfers between devices with their start and end apart: 12, of which 5 were waited for; matrix products, arithmetic and copies ran while one was open for 1% of the time, Pallas kernels for 37%

profile of v3, /device:TPU:0, one launch (start us, length us, event | category | flops | bytes accessed | tf_op | source)
XLA Modules:
  0.0 65.3 jit_solution(9904690248017716716)
XLA Ops:
  0.0 2.2 %states.2 = (bf16[528,128]{1,0:T(8,128)(2,1)S(1)}, f32[8,512]{1,0:T(8,128)}) custom-call(s32[1]{0:T(128)} %bitcast.4.which_ref, f32[8,512]{1,0:T(8,128)} %bitcast.8, bf16[512,1024]{1,0:T(8,128)(2,1)} %k_ref.7, bf16[512,1024]{1,0:T(8,128)(2,1)} %v_ref.7, bf16[512,1024]{1,0:T(8,128)(2,1)} %v_ref.7), custom_call_target="tpu_custom_call" | custom-call | tf_op jit(solution)/shard_map/states/pallas_call | solution.py:101
  2.2 1.9 %states.3 = (f32[528,128]{1,0:T(8,128)S(1)}, f32[8,512]{1,0:T(8,128)S(1)}) custom-call(s32[1]{0:T(128)} %bitcast.2.which_ref.side_ref, f32[8,512]{1,0:T(8,128)} %bitcast.9, bf16[512,1024]{1,0:T(8,128)(2,1)} %k_ref.7, bf16[512,1024]{1,0:T(8,128)(2,1)} %v_ref.7, bf16[528,128]{1,0:T(8,128)(2,1)S(1)} %get-tuple-element.37.hold_ref), custom_call_target="tpu_custom_call" | custom-call | tf_op jit(solution)/shard_map/states/pallas_call | solution.py:101
  4.1 0.6 collective-permute-start.5
  4.7 2.6 %collective-permute-start = (bf16[528,128]{1,0:T(8,128)(2,1)S(1)}, bf16[528,128]{1,0:T(8,128)(2,1)S(1)}, u32[]{:S(2)}, u32[]{:S(2)}) collective-permute-start(bf16[528,128]{1,0:T(8,128)(2,1)S(1)} %get-tuple-element.37.hold_ref), channel_id=1, source_target_pairs={{0,4},{4,0},{8,12},{12,8},{16,20},{20,16},{24,28},{28,24},{1,5},{5... | collective-permute-start | bytes 405512 | tf_op jit(solution)/shard_map/ppermute | solution.py:423
  7.2 4.2 %collective-permute-done.met_ref = bf16[528,128]{1,0:T(8,128)(2,1)S(1)} collective-permute-done((bf16[528,128]{1,0:T(8,128)(2,1)S(1)}, bf16[528,128]{1,0:T(8,128)(2,1)S(1)}, u32[]{:S(2)}, u32[]{:S(2)}) %collective-permute-start) | collective-permute-done | bytes 135200 | tf_op jit(solution)/shard_map/ppermute | solution.py:423
  11.4 0.1 pair.1
  11.5 3.8 %collective-permute-start.1 = (bf16[528,128]{1,0:T(8,128)(2,1)S(1)}, bf16[528,128]{1,0:T(8,128)(2,1)S(1)}, u32[]{:S(2)}, u32[]{:S(2)}) collective-permute-start(bf16[528,128]{1,0:T(8,128)(2,1)S(1)} %get-tuple-element.40.hold_ref), channel_id=1, source_target_pairs={{0,8},{4,12},{8,16},{12,20},{16,24},{20,28},{1,9},{5,13},{9,17},{1... | collective-permute-start | bytes 405512 | tf_op jit(solution)/shard_map/ppermute | solution.py:450
  15.2 4.5 %collective-permute-start.3 = (bf16[528,128]{1,0:T(8,128)(2,1)S(1)}, bf16[528,128]{1,0:T(8,128)(2,1)S(1)}, u32[]{:S(2)}, u32[]{:S(2)}) collective-permute-start(bf16[528,128]{1,0:T(8,128)(2,1)S(1)} %get-tuple-element.40.hold_ref), channel_id=1, source_target_pairs={{0,16},{4,20},{1,17},{5,21},{2,18},{6,22},{3,19},{7,23}} | collective-permute-start | bytes 405512 | tf_op jit(solution)/shard_map/ppermute | solution.py:454
  19.7 2.5 %local.4 = (f32[512,256]{1,0:T(8,128)S(1)}, bf16[512,256]{1,0:T(8,128)(2,1)S(1)}) custom-call(f32[8,512]{1,0:T(8,128)S(1)} %get-tuple-element.42.cum_ref, bf16[512,1024]{1,0:T(8,128)(2,1)} %q_ref.7, bf16[512,1024]{1,0:T(8,128)(2,1)} %k_ref.7, bf16[512,1024]{1,0:T(8,128)(2,1)} %v_ref.7, bf16[528,128]{1,0:T(8,128)(2,1)S(1)} %get-tuple-element.40.hold_ref), custom_call_target="tpu_custom_call" | custom-call | tf_op jit(solution)/shard_map/local/pallas_call | solution.py:313
  22.2 0.0 collective-permute-done.1.got_ref.early_ref
  22.2 0.8 %widen.1 = (bf16[528,128]{1,0:T(8,128)(2,1)S(1)}, f32[528,128]{1,0:T(8,128)}, f32[528,128]{1,0:T(8,128)S(1)}) custom-call(bf16[528,128]{1,0:T(8,128)(2,1)S(1)} %collective-permute-done.1.got_ref.early_ref, bf16[528,128]{1,0:T(8,128)(2,1)S(1)} %collective-permute-done.1.got_ref.early_ref, f32[528,128]{1,0:T(8,128)S(1)} %get-tuple-element.41.window_ref.before_ref, ...), custom_call_target="tpu_custom_call" | custom-call | tf_op jit(solution)/shard_map/widen/pallas_call | solution.py:209
  23.0 0.7 %collective-permute-start.2 = (bf16[528,128]{1,0:T(8,128)(2,1)S(1)}, bf16[528,128]{1,0:T(8,128)(2,1)S(1)}, u32[]{:S(2)}, u32[]{:S(2)}) collective-permute-start(bf16[528,128]{1,0:T(8,128)(2,1)S(1)} %get-tuple-element.44.hold_ref), channel_id=1, source_target_pairs={{8,24},{12,28},{9,25},{13,29},{10,26},{14,30},{11,27},{15,31}} | collective-permute-start | bytes 405512 | tf_op jit(solution)/shard_map/ppermute | solution.py:450
  23.6 2.5 %local.5 = (f32[512,256]{1,0:T(8,128)S(1)}, bf16[512,256]{1,0:T(8,128)(2,1)S(1)}) custom-call(f32[8,512]{1,0:T(8,128)S(1)} %get-tuple-element.42.cum_ref, bf16[512,1024]{1,0:T(8,128)(2,1)} %q_ref.7, bf16[512,1024]{1,0:T(8,128)(2,1)} %k_ref.7, bf16[512,1024]{1,0:T(8,128)(2,1)} %v_ref.7, bf16[528,128]{1,0:T(8,128)(2,1)S(1)} %get-tuple-element.44.hold_ref), custom_call_target="tpu_custom_call" | custom-call | tf_op jit(solution)/shard_map/local/pallas_call | solution.py:313
  26.1 2.5 %local.6 = (f32[512,256]{1,0:T(8,128)S(1)}, bf16[512,256]{1,0:T(8,128)(2,1)S(1)}) custom-call(f32[8,512]{1,0:T(8,128)S(1)} %get-tuple-element.42.cum_ref, bf16[512,1024]{1,0:T(8,128)(2,1)} %q_ref.7, bf16[512,1024]{1,0:T(8,128)(2,1)} %k_ref.7, bf16[512,1024]{1,0:T(8,128)(2,1)} %v_ref.7, f32[512,256]{1,0:T(8,128)S(1)} %get-tuple-element.47.hold_ref.refs_1_), custom_call_target="tpu_custom_call" | custom-call | tf_op jit(solution)/shard_map/local/pallas_call | solution.py:313
  28.6 0.0 collective-permute-done.3.early_ref
  28.6 0.0 collective-permute-done.2.got_ref
  28.6 0.1 enter.1
  28.7 1.6 %collective-permute-start.4 = (bf16[512,128]{1,0:T(8,128)(2,1)S(1)}, bf16[512,128]{1,0:T(8,128)(2,1)S(1)}, u32[]{:S(2)}, u32[]{:S(2)}) collective-permute-start(bf16[512,128]{1,0:T(8,128)(2,1)S(1)} %get-tuple-element.50.hold_ref), channel_id=1, source_target_pairs={{0,4},{4,0},{8,12},{12,8},{16,20},{20,16},{24,28},{28,24},{1,5},{5... | collective-permute-start | bytes 393224 | tf_op jit(solution)/shard_map/ppermute | solution.py:464
  30.3 0.1 pad_add_fusion.spot_ref
  30.3 0.0 collective-permute-done.5.refs_1_.far_ref
  30.3 3.7 %local.7 = (f32[512,256]{1,0:T(8,128)S(1)}, bf16[512,256]{1,0:T(8,128)(2,1)S(1)}, bf16[1024,512]{1,0:T(8,128)(2,1)S(1)}, bf16[1024,512]{1,0:T(8,128)(2,1)S(1)}) custom-call(f32[8,512]{1,0:T(8,128)S(1)} %get-tuple-element.42.cum_ref, bf16[512,1024]{1,0:T(8,128)(2,1)} %q_ref.7, bf16[512,1024]{1,0:T(8,128)(2,1)} %k_ref.7, bf16[512,1024]{1,0:T(8,128)(2,1)} %v_ref.7, ...), custom_call_target="tpu_custom_call" | custom-call | tf_op jit(solution)/shard_map/local/pallas_call | solution.py:313
  34.1 0.0 collective-permute-done.4.met_ref
  34.1 1.1 %norm_away.1 = bf16[256,1024]{1,0:T(8,128)(2,1)S(1)} custom-call(s32[3]{0:T(128)S(1)} %pad_add_fusion.spot_ref, bf16[512,128]{1,0:T(8,128)(2,1)S(1)} %get-tuple-element.49.mine_ref, bf16[512,128]{1,0:T(8,128)(2,1)S(1)} %collective-permute-done.4.met_ref, f32[1,1024]{1,0:T(1,128)S(1)} %bitcast.6, f32[512,256]{1,0:T(8,128)S(1)} %get-tuple-element.43.hold_ref.refs_0_, ...), custom_call_target="tpu_custom_call" | custom-call | tf_op jit(solution)/shard_map/norm_away/pallas_call | solution.py:359
  35.2 0.1 collective-permute-start.6
  35.2 1.1 %norm_home.1.mine_ref.hold_ref = bf16[256,1024]{1,0:T(8,128)(2,1)S(1)} custom-call(s32[3]{0:T(128)S(1)} %pad_add_fusion.spot_ref, bf16[512,128]{1,0:T(8,128)(2,1)S(1)} %get-tuple-element.49.mine_ref, bf16[512,128]{1,0:T(8,128)(2,1)S(1)} %collective-permute-done.4.met_ref, f32[1,1024]{1,0:T(1,128)S(1)} %bitcast.7, ...), custom_call_target="tpu_custom_call" | custom-call | tf_op jit(solution)/shard_map/norm_home/pallas_call | solution.py:359
  36.3 0.8 %collective-permute-done.6.other_ref = bf16[256,1024]{1,0:T(8,128)(2,1)S(1)} collective-permute-done((bf16[256,1024]{1,0:T(8,128)(2,1)S(1)}, bf16[256,1024]{1,0:T(8,128)(2,1)S(1)}, u32[]{:S(2)}, u32[]{:S(2)}) %collective-permute-start.6) | collective-permute-done | bytes 524320 | tf_op jit(solution)/shard_map/ppermute | solution.py:472
  37.1 0.7 %project.5 = (f32[128,512]{1,0:T(8,128)S(1)}, bf16[128,512]{1,0:T(8,128)(2,1)S(1)}) custom-call(bf16[256,1024]{1,0:T(8,128)(2,1)S(1)} %norm_home.1.mine_ref.hold_ref, bf16[256,1024]{1,0:T(8,128)(2,1)S(1)} %collective-permute-done.6.other_ref, bf16[1024,512]{1,0:T(8,128)(2,1)S(1)} %get-tuple-element.57.near_ref, ...), custom_call_target="tpu_custom_call" | custom-call | tf_op jit(solution)/shard_map/project/pallas_call | solution.py:383
  37.9 1.6 %collective-permute-start.7 = (bf16[128,512]{1,0:T(8,128)(2,1)S(1)}, bf16[128,512]{1,0:T(8,128)(2,1)S(1)}, u32[]{:S(2)}, u32[]{:S(2)}) collective-permute-start(bf16[128,512]{1,0:T(8,128)(2,1)S(1)} %get-tuple-element.60.hold_ref), channel_id=1, source_target_pairs={{0,2},{1,3},{2,0},{3,1},{4,6},{5,7},{6,4},{7,5},{8,10},{9,11},{10,... | collective-permute-start | bytes 393224 | tf_op jit(solution)/shard_map/ppermute | solution.py:487
  39.4 3.0 %project.6 = (f32[128,1024]{1,0:T(8,128)S(1)}, bf16[128,1024]{1,0:T(8,128)(2,1)S(1)}) custom-call(bf16[256,1024]{1,0:T(8,128)(2,1)S(1)} %norm_home.1.mine_ref.hold_ref, bf16[256,1024]{1,0:T(8,128)(2,1)S(1)} %collective-permute-done.6.other_ref, bf16[1024,4096]{1,0:T(8,128)(2,1)} %near_ref.7, bf16[1024,4096]{1,0:T(8,128)(2,1)} %collective-permute-done.5.refs_1_.far_ref, ...), custom_call_target="tpu_custom_call" | custom-call | tf_op jit(solution)/shard_map/project/pallas_call | solution.py:383
  42.5 0.6 collective-permute-start.8
  43.0 3.0 %project.7 = (f32[128,1024]{1,0:T(8,128)S(1)}, bf16[128,1024]{1,0:T(8,128)(2,1)S(1)}) custom-call(bf16[256,1024]{1,0:T(8,128)(2,1)S(1)} %norm_home.1.mine_ref.hold_ref, bf16[256,1024]{1,0:T(8,128)(2,1)S(1)} %collective-permute-done.6.other_ref, bf16[1024,4096]{1,0:T(8,128)(2,1)} %near_ref.7, bf16[1024,4096]{1,0:T(8,128)(2,1)} %collective-permute-done.5.refs_1_.far_ref, ...), custom_call_target="tpu_custom_call" | custom-call | tf_op jit(solution)/shard_map/project/pallas_call | solution.py:383
  46.1 1.6 %collective-permute-start.9 = (bf16[128,1024]{1,0:T(8,128)(2,1)S(1)}, bf16[128,1024]{1,0:T(8,128)(2,1)S(1)}, u32[]{:S(2)}, u32[]{:S(2)}) collective-permute-start(bf16[128,1024]{1,0:T(8,128)(2,1)S(1)} %get-tuple-element.64.hold_ref), channel_id=1, source_target_pairs={{0,2},{1,3},{2,0},{3,1},{4,6},{5,7},{6,4},{7,5},{8,10},{9,11},{10,... | collective-permute-start | bytes 786440 | tf_op jit(solution)/shard_map/ppermute | solution.py:487
  47.7 3.0 %project.8 = (f32[128,1024]{1,0:T(8,128)S(1)}, bf16[128,1024]{1,0:T(8,128)(2,1)S(1)}) custom-call(bf16[256,1024]{1,0:T(8,128)(2,1)S(1)} %norm_home.1.mine_ref.hold_ref, bf16[256,1024]{1,0:T(8,128)(2,1)S(1)} %collective-permute-done.6.other_ref, bf16[1024,4096]{1,0:T(8,128)(2,1)} %near_ref.7, bf16[1024,4096]{1,0:T(8,128)(2,1)} %collective-permute-done.5.refs_1_.far_ref, ...), custom_call_target="tpu_custom_call" | custom-call | tf_op jit(solution)/shard_map/project/pallas_call | solution.py:383
  50.7 0.0 copy-start.1
  50.7 0.6 collective-permute-start.10
  51.3 2.2 %project.9 = (f32[128,512]{1,0:T(8,128)S(1)}, bf16[128,512]{1,0:T(8,128)(2,1)S(1)}) custom-call(bf16[256,1024]{1,0:T(8,128)(2,1)S(1)} %norm_home.1.mine_ref.hold_ref, bf16[256,1024]{1,0:T(8,128)(2,1)S(1)} %collective-permute-done.6.other_ref, bf16[1024,4096]{1,0:T(8,128)(2,1)} %near_ref.7, bf16[1024,4096]{1,0:T(8,128)(2,1)} %collective-permute-done.5.refs_1_.far_ref, ...), custom_call_target="tpu_custom_call" | custom-call | tf_op jit(solution)/shard_map/project/pallas_call | solution.py:383
  53.6 1.6 %collective-permute-start.11 = (bf16[128,512]{1,0:T(8,128)(2,1)S(1)}, bf16[128,512]{1,0:T(8,128)(2,1)S(1)}, u32[]{:S(2)}, u32[]{:S(2)}) collective-permute-start(bf16[128,512]{1,0:T(8,128)(2,1)S(1)} %get-tuple-element.68), channel_id=1, source_target_pairs={{0,2},{1,3},{2,0},{3,1},{4,6},{5,7},{6,4},{7,5},{8,10},{9,11},{10,... | collective-permute-start | bytes 393224 | tf_op jit(solution)/shard_map/ppermute | solution.py:487
  55.1 0.0 collective-permute-done.7
  55.2 0.1 dynamic_update_slice.15
  55.3 0.0 collective-permute-done.8
  55.3 0.1 fusion
  55.4 1.9 %collective-permute-done.9 = bf16[128,1024]{1,0:T(8,128)(2,1)S(1)} collective-permute-done((bf16[128,1024]{1,0:T(8,128)(2,1)S(1)}, bf16[128,1024]{1,0:T(8,128)(2,1)S(1)}, u32[]{:S(2)}, u32[]{:S(2)}) %collective-permute-start.9) | collective-permute-done | bytes 262176 | tf_op jit(solution)/shard_map/ppermute | solution.py:487
  57.3 0.1 fusion.1
  57.4 5.5 %collective-permute-done.10 = bf16[128,1024]{1,0:T(8,128)(2,1)S(1)} collective-permute-done((bf16[128,1024]{1,0:T(8,128)(2,1)S(1)}, bf16[128,1024]{1,0:T(8,128)(2,1)S(1)}, u32[]{:S(2)}, u32[]{:S(2)}) %collective-permute-start.10) | collective-permute-done | bytes 262176 | tf_op jit(solution)/shard_map/ppermute | solution.py:487
  62.9 0.1 fusion.2
  63.0 0.0 copy-start.2
  63.0 1.6 %collective-permute-done.11 = bf16[128,512]{1,0:T(8,128)(2,1)S(1)} collective-permute-done((bf16[128,512]{1,0:T(8,128)(2,1)S(1)}, bf16[128,512]{1,0:T(8,128)(2,1)S(1)}, u32[]{:S(2)}, u32[]{:S(2)}) %collective-permute-start.11) | collective-permute-done | bytes 131104 | tf_op jit(solution)/shard_map/ppermute | solution.py:487
  64.6 0.7 %fusion.3 = bf16[128,4096]{1,0:T(8,128)(2,1)} fusion(bf16[128,4096]{1,0:T(8,128)(2,1)} %copy-done.2, bf16[128,512]{1,0:T(8,128)(2,1)S(1)} %collective-permute-done.11, f32[128,512]{1,0:T(8,128)S(1)} %get-tuple-element.67, bf16[128,4096]{1,0:T(8,128)(2,1)S(1)} %copy-done.1), kind=kLoop, calls=%fused_computation.8 | loop fusion | flops 327680 | bytes 655360 | tf_op jit(solution)/shard_map/dynamic_update_slice | solution.py:488
  (5 shorter events, 0.1 us)
Async XLA Ops:
  4.1 26.2 %collective-permute-start.5 = (bf16[1024,4096]{1,0:T(8,128)(2,1)}, bf16[1024,4096]{1,0:T(8,128)(2,1)}, u32[]{:S(2)}, u32[]{:S(2)}) collective-permute-start(bf16[1024,4096]{1,0:T(8,128)(2,1)} %near_ref.7), channel_id=1, source_target_pairs={{0,1},{1,0},{2,3},{3,2},{4,5},{5,4},{6,7},{7,6},{8,9},{9,8},{10,11... | collective-permute-start | bytes 25165832 | tf_op jit(solution)/shard_map/ppermute | solution.py:427
  4.7 6.7 %collective-permute-start = (bf16[528,128]{1,0:T(8,128)(2,1)S(1)}, bf16[528,128]{1,0:T(8,128)(2,1)S(1)}, u32[]{:S(2)}, u32[]{:S(2)}) collective-permute-start(bf16[528,128]{1,0:T(8,128)(2,1)S(1)} %get-tuple-element.37.hold_ref), channel_id=1, source_target_pairs={{0,4},{4,0},{8,12},{12,8},{16,20},{20,16},{24,28},{28,24},{1,5},{5... | collective-permute-start | bytes 405512 | tf_op jit(solution)/shard_map/ppermute | solution.py:423
  11.5 10.7 %collective-permute-start.1 = (bf16[528,128]{1,0:T(8,128)(2,1)S(1)}, bf16[528,128]{1,0:T(8,128)(2,1)S(1)}, u32[]{:S(2)}, u32[]{:S(2)}) collective-permute-start(bf16[528,128]{1,0:T(8,128)(2,1)S(1)} %get-tuple-element.40.hold_ref), channel_id=1, source_target_pairs={{0,8},{4,12},{8,16},{12,20},{16,24},{20,28},{1,9},{5,13},{9,17},{1... | collective-permute-start | bytes 405512 | tf_op jit(solution)/shard_map/ppermute | solution.py:450
  15.2 13.3 %collective-permute-start.3 = (bf16[528,128]{1,0:T(8,128)(2,1)S(1)}, bf16[528,128]{1,0:T(8,128)(2,1)S(1)}, u32[]{:S(2)}, u32[]{:S(2)}) collective-permute-start(bf16[528,128]{1,0:T(8,128)(2,1)S(1)} %get-tuple-element.40.hold_ref), channel_id=1, source_target_pairs={{0,16},{4,20},{1,17},{5,21},{2,18},{6,22},{3,19},{7,23}} | collective-permute-start | bytes 405512 | tf_op jit(solution)/shard_map/ppermute | solution.py:454
  23.0 5.6 %collective-permute-start.2 = (bf16[528,128]{1,0:T(8,128)(2,1)S(1)}, bf16[528,128]{1,0:T(8,128)(2,1)S(1)}, u32[]{:S(2)}, u32[]{:S(2)}) collective-permute-start(bf16[528,128]{1,0:T(8,128)(2,1)S(1)} %get-tuple-element.44.hold_ref), channel_id=1, source_target_pairs={{8,24},{12,28},{9,25},{13,29},{10,26},{14,30},{11,27},{15,31}} | collective-permute-start | bytes 405512 | tf_op jit(solution)/shard_map/ppermute | solution.py:450
  28.7 5.4 %collective-permute-start.4 = (bf16[512,128]{1,0:T(8,128)(2,1)S(1)}, bf16[512,128]{1,0:T(8,128)(2,1)S(1)}, u32[]{:S(2)}, u32[]{:S(2)}) collective-permute-start(bf16[512,128]{1,0:T(8,128)(2,1)S(1)} %get-tuple-element.50.hold_ref), channel_id=1, source_target_pairs={{0,4},{4,0},{8,12},{12,8},{16,20},{20,16},{24,28},{28,24},{1,5},{5... | collective-permute-start | bytes 393224 | tf_op jit(solution)/shard_map/ppermute | solution.py:464
  30.3 3.7 %copy-start = (f32[1024]{0:T(1024)S(1)}, f32[1024]{0:T(1024)}, u32[]{:S(2)}) copy-start(f32[1024]{0:T(1024)} %param.11) | copy-start | bytes 12292
  35.2 2.0 %collective-permute-start.6 = (bf16[256,1024]{1,0:T(8,128)(2,1)S(1)}, bf16[256,1024]{1,0:T(8,128)(2,1)S(1)}, u32[]{:S(2)}, u32[]{:S(2)}) collective-permute-start(bf16[256,1024]{1,0:T(8,128)(2,1)S(1)} %norm_away.1), channel_id=1, source_target_pairs={{0,1},{1,0},{2,3},{3,2},{4,5},{5,4},{6,7},{7,6},{8,9},{9,8},{10,11... | collective-permute-start | bytes 1572872 | tf_op jit(solution)/shard_map/ppermute | solution.py:472
  37.9 17.3 %collective-permute-start.7 = (bf16[128,512]{1,0:T(8,128)(2,1)S(1)}, bf16[128,512]{1,0:T(8,128)(2,1)S(1)}, u32[]{:S(2)}, u32[]{:S(2)}) collective-permute-start(bf16[128,512]{1,0:T(8,128)(2,1)S(1)} %get-tuple-element.60.hold_ref), channel_id=1, source_target_pairs={{0,2},{1,3},{2,0},{3,1},{4,6},{5,7},{6,4},{7,5},{8,10},{9,11},{10,... | collective-permute-start | bytes 393224 | tf_op jit(solution)/shard_map/ppermute | solution.py:487
  42.5 12.8 %collective-permute-start.8 = (bf16[128,1024]{1,0:T(8,128)(2,1)S(1)}, bf16[128,1024]{1,0:T(8,128)(2,1)S(1)}, u32[]{:S(2)}, u32[]{:S(2)}) collective-permute-start(bf16[128,1024]{1,0:T(8,128)(2,1)S(1)} %get-tuple-element.62.hold_ref), channel_id=1, source_target_pairs={{0,2},{1,3},{2,0},{3,1},{4,6},{5,7},{6,4},{7,5},{8,10},{9,11},{10,... | collective-permute-start | bytes 786440 | tf_op jit(solution)/shard_map/ppermute | solution.py:487
  46.1 11.2 %collective-permute-start.9 = (bf16[128,1024]{1,0:T(8,128)(2,1)S(1)}, bf16[128,1024]{1,0:T(8,128)(2,1)S(1)}, u32[]{:S(2)}, u32[]{:S(2)}) collective-permute-start(bf16[128,1024]{1,0:T(8,128)(2,1)S(1)} %get-tuple-element.64.hold_ref), channel_id=1, source_target_pairs={{0,2},{1,3},{2,0},{3,1},{4,6},{5,7},{6,4},{7,5},{8,10},{9,11},{10,... | collective-permute-start | bytes 786440 | tf_op jit(solution)/shard_map/ppermute | solution.py:487
  50.7 4.4 %copy-start.1 = (bf16[128,4096]{1,0:T(8,128)(2,1)S(1)}, bf16[128,4096]{1,0:T(8,128)(2,1)}, u32[]{:S(2)}) copy-start(bf16[128,4096]{1,0:T(8,128)(2,1)} %param.13) | copy-start | bytes 3145732
  50.7 12.2 %collective-permute-start.10 = (bf16[128,1024]{1,0:T(8,128)(2,1)S(1)}, bf16[128,1024]{1,0:T(8,128)(2,1)S(1)}, u32[]{:S(2)}, u32[]{:S(2)}) collective-permute-start(bf16[128,1024]{1,0:T(8,128)(2,1)S(1)} %get-tuple-element.66.hold_ref), channel_id=1, source_target_pairs={{0,2},{1,3},{2,0},{3,1},{4,6},{5,7},{6,4},{7,5},{8,10},{9,11},{10,... | collective-permute-start | bytes 786440 | tf_op jit(solution)/shard_map/ppermute | solution.py:487
  53.6 11.1 %collective-permute-start.11 = (bf16[128,512]{1,0:T(8,128)(2,1)S(1)}, bf16[128,512]{1,0:T(8,128)(2,1)S(1)}, u32[]{:S(2)}, u32[]{:S(2)}) collective-permute-start(bf16[128,512]{1,0:T(8,128)(2,1)S(1)} %get-tuple-element.68), channel_id=1, source_target_pairs={{0,2},{1,3},{2,0},{3,1},{4,6},{5,7},{6,4},{7,5},{8,10},{9,11},{10,... | collective-permute-start | bytes 393224 | tf_op jit(solution)/shard_map/ppermute | solution.py:487
  63.0 1.6 %copy-start.2 = (bf16[128,4096]{1,0:T(8,128)(2,1)}, bf16[128,4096]{1,0:T(8,128)(2,1)S(1)}, u32[]{:S(2)}) copy-start(bf16[128,4096]{1,0:T(8,128)(2,1)S(1)} %fusion.2) | copy-start | bytes 3145732
